TPU v7x, 128 devices: a whole 4x4x4 slice. The times are simulated.
128 devices in a mesh: blk: 128 (over z, x, y, core).
Axes of the slice: x: 4, y: 4, z: 4, core: 2. Of those that a mesh axis runs over, the one named last changes fastest.
Arguments:
- state: float32 [4, 2048, 128, 256], P(None, 'blk'), may hold values from -6 to 6
- sample_cell: int32 [65536], P('blk'), may hold values from 0 to 491262, as said below
- sample_frac: float32 [3, 65536], P(None, 'blk'), may hold values from 0 to 1
- sample_owner: int32 [65536, 1], P('blk'), may hold values from 0 to 127; in each aligned block of 512 rows (0 to 511, 512 to 1023, ...) at most 8 rows name the same one
- face_angles: float32 [2, 131072], P(None, 'blk'), may hold values from -3.140625 to 3.140625
- face_height: float32 [131072], P('blk'), may hold values from 0.05 to 0.5
- wall_temp: float32 [131072], P('blk'), may hold values from -6 to 6
- face_visc: float32 [131072], P('blk'), may hold values from 0.005 to 0.05
Outputs:
- final_state: float32 [4, 2048, 128, 256], P(None, 'blk')
- wall_flux: float32 [4, 65536], P(None, 'blk')
Inputs may be any that keep to these rules, and one draw needn't show every extreme that they name: `sample_cell`: index i * 128 * 256 + j * 256 + k with i < 15, j < 127, k < 255, so that the whole block lies in the partition. `sample_owner`: among the 512 exchange points of one partition no owner is named more than 8 times, a bound that some block reaches.
All inputs are finite; a program needn't handle non-finite values.
Results may differ from a plain program's by a relative error of at most 0.0003.
Values sent between devices are 32-bit elements; how exact they have to be, the bound alone decides.
No kernel may reach another device: no remote copies, remote signals or barrier semaphores. Data moves between devices by JAX's collectives and lax.ppermute only.
A program may use at most 128 MiB of HBM per device.

v0:
```python
import jax
import jax.numpy as jnp
from jax import lax
from jax.sharding import PartitionSpec as P

NPTS = 64
NEWTON = 3


time_step = 0.1
grid_viscosity = 0.2
karman = 0.41
prandtl = 0.72
turb_prandtl = 0.9
speed_floor = 0.5


def extended(cells, sides, width):
    for axis, dim in sides:
        count = lax.axis_size(axis)
        head = lax.slice_in_dim(cells, 0, width, axis=dim)
        tail = lax.slice_in_dim(cells, cells.shape[dim] - width, cells.shape[dim], axis=dim)
        cells = jnp.concatenate(
            [
                lax.ppermute(tail, axis, [(i, (i + 1) % count) for i in range(count)]),
                cells,
                lax.ppermute(head, axis, [((i + 1) % count, i) for i in range(count)]),
            ],
            axis=dim,
        )
    return cells


def transport(padded):
    center = padded[:, 1:-1]
    velocity = center[0:3]
    framed = jnp.pad(center, ((0, 0), (0, 0), (1, 1), (1, 1)))
    east_side = padded[:, 2:]
    west_side = padded[:, :-2]
    north_side = framed[:, :, 2:, 1:-1]
    south_side = framed[:, :, :-2, 1:-1]
    upper_side = framed[:, :, 1:-1, 2:]
    lower_side = framed[:, :, 1:-1, :-2]
    advect = (
        velocity[0] * (east_side - west_side)
        + velocity[1] * (north_side - south_side)
        + velocity[2] * (upper_side - lower_side)
    )
    spread = (
        east_side + west_side + north_side + south_side + upper_side + lower_side - 6.0 * center
    )
    return -0.5 * advect + grid_viscosity * spread


def with_rims(field):
    return extended(field, (("blk", 1),), 1)


def corner_factor(fraction, upper_flag):
    if upper_flag:
        return fraction
    return 1.0 - fraction


def sample_lines(middle, sample_cell, sample_frac):
    span_cells = middle.shape[2]
    line_cells = middle.shape[3]
    points = sample_cell.shape[0]
    lines = middle.reshape(4, -1, line_cells)
    base_line = sample_cell // line_cells
    offset = sample_cell - base_line * line_cells
    line_ids = []
    plane_weights = []
    for step_x in (0, 1):
        for step_y in (0, 1):
            line_ids.append(base_line + step_x * span_cells + step_y)
            plane_weights.append(
                corner_factor(sample_frac[0], step_x) * corner_factor(sample_frac[1], step_y)
            )
    line_ids = jnp.stack(line_ids).reshape(-1)
    plane_weights = jnp.stack(plane_weights)
    picked = jnp.take(lines, line_ids, axis=1).reshape(4, 4, points, line_cells)
    along = lax.broadcasted_iota(jnp.int32, (points, line_cells), 1)
    lower_hit = (along == offset[:, None]).astype(jnp.float32)
    upper_hit = (along == offset[:, None] + 1).astype(jnp.float32)
    depth_weights = (
        lower_hit * (1.0 - sample_frac[2])[:, None] + upper_hit * sample_frac[2][:, None]
    )
    along_line = jnp.sum(picked * depth_weights[None, None], axis=3)
    return jnp.sum(along_line * plane_weights[None], axis=1)


def slot_index(owners, groups, capacity):
    onehot = (owners[:, None] == jnp.arange(groups, dtype=jnp.int32)[None, :]).astype(jnp.int32)
    before = jnp.cumsum(onehot, axis=0) - onehot
    position = jnp.sum(before * onehot, axis=1)
    return owners * capacity + position


def pick_slots(table, slot_table):
    return lax.dot_general(
        table,
        slot_table,
        (((1,), (1,)), ((), ())),
        precision=lax.Precision.HIGHEST,
        preferred_element_type=jnp.float32,
    )


def wall_model(sample, angles, height, wall_temp, viscosity):
    normal = jnp.stack(
        [
            jnp.sin(angles[0]) * jnp.cos(angles[1]),
            jnp.sin(angles[0]) * jnp.sin(angles[1]),
            jnp.cos(angles[0]),
        ]
    )
    normal_speed = jnp.sum(sample[0:3] * normal, axis=0)
    tangent = sample[0:3] - normal_speed[None] * normal
    tangent_speed = jnp.maximum(jnp.sqrt(jnp.sum(tangent * tangent, axis=0)), speed_floor)
    direction = tangent / tangent_speed[None]
    ladder = (jnp.arange(NPTS, dtype=jnp.float32) + 0.5) / NPTS
    heights = height[None] * (ladder * ladder)[:, None]
    quad_weights = height[None] * (2.0 * ladder / NPTS)[:, None]
    friction = jnp.sqrt(viscosity * tangent_speed / height)
    for newton_step in range(NEWTON):
        eddy_visc = viscosity[None] + karman * heights * friction[None]
        inverse_sum = jnp.sum(quad_weights / eddy_visc, axis=0)
        slope_sum = jnp.sum(quad_weights * karman * heights / (eddy_visc * eddy_visc), axis=0)
        residual = friction * friction * inverse_sum - tangent_speed
        derivative = 2.0 * friction * inverse_sum - friction * friction * slope_sum
        friction = friction - residual / derivative
    conduct = viscosity[None] / prandtl + karman * heights * friction[None] / turb_prandtl
    resist = jnp.sum(quad_weights / conduct, axis=0)
    heat_flux = (sample[3] - wall_temp) / resist
    stress = (friction * friction)[None] * direction
    return jnp.concatenate([stress, heat_flux[None]], axis=0)


def on_device(
    state, sample_cell, sample_frac, sample_owner, face_angles, face_height, wall_temp, face_visc
):
    groups = lax.axis_size("blk")
    capacity = face_height.shape[0] // groups
    middle = state + time_step * transport(with_rims(state))
    final_state = 0.5 * state + 0.5 * (middle + time_step * transport(with_rims(middle)))
    sampled = sample_lines(middle, sample_cell, sample_frac)
    slots = slot_index(sample_owner[:, 0], groups, capacity)
    slot_table = (slots[:, None] == jnp.arange(groups * capacity, dtype=jnp.int32)[None, :]).astype(
        jnp.float32
    )
    outgoing = jnp.dot(
        sampled, slot_table, precision=lax.Precision.HIGHEST, preferred_element_type=jnp.float32
    )
    incoming = lax.all_to_all(outgoing, "blk", split_axis=1, concat_axis=1, tiled=True)
    solved = wall_model(incoming, face_angles, face_height, wall_temp, face_visc)
    returned = lax.all_to_all(solved, "blk", split_axis=1, concat_axis=1, tiled=True)
    wall_flux = pick_slots(returned, slot_table)
    return (final_state, wall_flux)


def solution(mesh):
    placed = (
        P(None, "blk", None, None),
        P("blk"),
        P(None, "blk"),
        P("blk", None),
        P(None, "blk"),
        P("blk"),
        P("blk"),
        P("blk"),
    )
    return jax.shard_map(
        on_device,
        mesh=mesh,
        in_specs=placed,
        out_specs=(P(None, "blk", None, None), P(None, "blk")),
        check_vma=False,
    )
```

profile of v0, /device:TPU:1, one launch (start us, length us, event | category | flops | bytes accessed | tf_op | source)
XLA Modules:
  0.0 188.3 jit_solution(6805822651793586209)
XLA Ops:
  0.6 2.3 %fusion.37 = (f32[4,1,128,256]{3,2,1,0:T(8,128)}, f32[4,1,128,256]{3,2,1,0:T(8,128)}) fusion(f32[4,16,128,256]{3,2,1,0:T(8,128)} %param.8), kind=kLoop, calls=%fused_computation.128 | loop fusion | bytes 2097152 | tf_op jit(solution)/shard_map/slice | solution.py:22
  2.9 1.4 collective-permute-start
  4.3 1.3 collective-permute-start.1
  5.6 0.7 broadcast_add_fusion.3
  6.4 0.8 subtract_multiply_fusion.1
  7.2 0.8 copy.62
  8.3 0.9 fusion.25
  9.2 0.7 multiply_add_fusion.2
  9.9 1.0 cosine_reduce_fusion
  11.3 0.3 select_add_fusion
  11.7 5.6 %slice_bitcast_fusion.5 = (f32[16,128,256]{2,1,0:T(8,128)S(1)}, f32[16,128,256]{2,1,0:T(8,128)}, f32[16,128,256]{2,1,0:T(8,128)}) fusion(f32[4,16,128,256]{3,2,1,0:T(8,128)} %param.8), kind=kLoop, calls=%fused_computation.22 | loop fusion | bytes 12582912 | tf_op jit(solution)/shard_map/mul | solution.py:45
  17.3 26.2 %multiply_add_fusion = f32[4,16,128,256]{3,2,1,0:T(8,128)} fusion(f32[4,16,128,256]{3,2,1,0:T(8,128)} %param.8, f32[4,1,128,256]{3,2,1,0:T(8,128)S(1)} %collective-permute-done, f32[4,1,128,256]{3,2,1,0:T(8,128)} %collective-permute-done.1, f32[16,128,256]{2,1,0:T(8,128)} %get-tuple-element.26, f32[16,128,256]{2,1,0:T(8,128)} %get-tuple-element.27, ...), kind=kLoop, calls=%fused_computation.15 | loop fusion | flops 46137344 | bytes 24117248 | tf_op jit(solution)/shard_map/add | solution.py:145
  43.4 12.4 %copy.60 = f32[4,16,128,256]{3,0,2,1:T(4,128)} copy(f32[4,16,128,256]{3,2,1,0:T(8,128)} %multiply_add_fusion) | data formatting | bytes 16777216 | tf_op jit(solution)/shard_map/add | solution.py:145
  55.8 22.2 %gather_fusion = f32[2048,4,256]{2,1,0:T(4,128)} fusion(f32[4,2048,256]{2,0,1:T(4,128)} %bitcast.53, s32[2048]{0:T(1024)S(1)} %broadcast_clamp_fusion), kind=kCustom, calls=%fused_computation | custom fusion | bytes 16785408 | tf_op jit(solution)/shard_map/jit(_take)/gather | solution.py:82
  78.1 30.1 %multiply_reduce_fusion = f32[2048,4]{1,0:T(8,128)S(1)} fusion(f32[2048,4,256]{2,1,0:T(4,128)} %gather_fusion, f32[2048,256]{1,0:T(8,128)S(1)} %bitcast.54, pred[2048]{0:T(1024)(128)(4,1)S(1)} %compare_and_fusion), kind=kLoop, calls=%fused_computation.13 | loop fusion | flops 6283264 | bytes 10520576 | tf_op jit(solution)/shard_map/reduce_sum | solution.py:89
  108.3 0.3 copy.61
  108.6 1.0 fusion.1
  109.7 0.9 copy.64
  110.5 15.0 %all-to-all-start = ((f32[4,128,8]{2,0,1:T(4,128)}), f32[4,128,8]{2,0,1:T(4,128)S(1)}, u32[]{:S(2)}, u32[]{:S(2)}) async-start(f32[4,128,8]{2,0,1:T(4,128)} %copy.64), calls=%async_computation | async-start | bytes 524288 | tf_op jit(solution)/shard_map/all_to_all | solution.py:155
  125.5 2.3 %fusion.36 = (f32[4,1,128,256]{3,2,1,0:T(8,128)}, f32[4,1,128,256]{3,2,1,0:T(8,128)}) fusion(f32[4,16,128,256]{3,2,1,0:T(8,128)} %multiply_add_fusion), kind=kLoop, calls=%fused_computation.127 | loop fusion | bytes 2097152 | tf_op jit(solution)/shard_map/slice | solution.py:22
  127.8 1.1 collective-permute-start.2
  128.9 0.7 collective-permute-start.3
  129.6 7.0 %all-to-all-done = f32[4,128,8]{2,0,1:T(4,128)S(1)} async-done(((f32[4,128,8]{2,0,1:T(4,128)}), f32[4,128,8]{2,0,1:T(4,128)S(1)}, u32[]{:S(2)}, u32[]{:S(2)}) %all-to-all-start) | async-done | bytes 16416 | tf_op jit(solution)/shard_map/all_to_all | solution.py:155
  137.0 0.2 fusion.11
  137.3 0.2 fusion.15
  137.5 0.2 fusion.19
  138.5 0.9 copy.69
  139.4 7.4 %all-to-all-start.1 = ((f32[4,128,8]{2,0,1:T(4,128)}), f32[4,128,8]{2,0,1:T(4,128)S(1)}, u32[]{:S(2)}, u32[]{:S(2)}) async-start(f32[4,128,8]{2,0,1:T(4,128)} %copy.69), calls=%async_computation.1 | async-start | bytes 524288 | tf_op jit(solution)/shard_map/all_to_all | solution.py:157
  146.8 5.5 %slice_bitcast_fusion.2 = (f32[16,128,256]{2,1,0:T(8,128)S(1)}, f32[16,128,256]{2,1,0:T(8,128)}, f32[16,128,256]{2,1,0:T(8,128)}) fusion(f32[4,16,128,256]{3,2,1,0:T(8,128)} %multiply_add_fusion), kind=kLoop, calls=%fused_computation.18 | loop fusion | bytes 12582912 | tf_op jit(solution)/shard_map/mul | solution.py:45
  152.2 5.6 %all-to-all-done.1 = f32[4,128,8]{2,0,1:T(4,128)S(1)} async-done(((f32[4,128,8]{2,0,1:T(4,128)}), f32[4,128,8]{2,0,1:T(4,128)S(1)}, u32[]{:S(2)}, u32[]{:S(2)}) %all-to-all-start.1) | async-done | bytes 16416 | tf_op jit(solution)/shard_map/all_to_all | solution.py:157
  158.0 1.7 fusion
  159.7 28.5 %add_multiply_fusion = f32[4,16,128,256]{3,2,1,0:T(8,128)} fusion(f32[4,16,128,256]{3,2,1,0:T(8,128)} %param.8, f32[4,16,128,256]{3,2,1,0:T(8,128)} %multiply_add_fusion, f32[4,1,128,256]{3,2,1,0:T(8,128)S(1)} %collective-permute-done.2, f32[4,1,128,256]{3,2,1,0:T(8,128)} %collective-permute-done.3, f32[16,128,256]{2,1,0:T(8,128)} %get-tuple-element.22, ...), kind=kLoop, calls=%fused_computation.14 | loop fusion | flops 50331648 | bytes 32505856 | tf_op jit(solution)/shard_map/add | solution.py:146
  (57 shorter events, 2.1 us)
Async XLA Ops:
  2.9 14.3 %collective-permute-start = (f32[4,1,128,256]{3,2,1,0:T(8,128)}, f32[4,1,128,256]{3,2,1,0:T(8,128)S(1)}, u32[]{:S(2)}, u32[]{:S(2)}) collective-permute-start(f32[4,1,128,256]{3,2,1,0:T(8,128)} %get-tuple-element.29), channel_id=1, source_target_pairs={{1,0},{2,1},{3,2},{4,3},{5,4},{6,5},{7,6},{8,7},{9,8},{10,9},{11,1... | collective-permute-start | bytes 1572872 | tf_op jit(solution)/shard_map/ppermute | solution.py:27
  4.3 12.9 %collective-permute-start.1 = (f32[4,1,128,256]{3,2,1,0:T(8,128)}, f32[4,1,128,256]{3,2,1,0:T(8,128)}, u32[]{:S(2)}, u32[]{:S(2)}) collective-permute-start(f32[4,1,128,256]{3,2,1,0:T(8,128)} %get-tuple-element.28), channel_id=1, source_target_pairs={{0,1},{1,2},{2,3},{3,4},{4,5},{5,6},{6,7},{7,8},{8,9},{9,10},{10,1... | collective-permute-start | bytes 1572872 | tf_op jit(solution)/shard_map/ppermute | solution.py:25
  78.1 58.8 %copy-start = (f32[1024]{0:T(1024)S(1)}, f32[1024]{0:T(1024)}, u32[]{:S(2)}) copy-start(f32[1024]{0:T(1024)} %param.13) | copy-start | bytes 12292
  78.1 58.8 %copy-start.1 = (f32[1024]{0:T(1024)S(1)}, f32[1024]{0:T(1024)}, u32[]{:S(2)}) copy-start(f32[1024]{0:T(1024)} %param.15) | copy-start | bytes 12292
  78.1 60.2 %copy-start.2 = (f32[1024]{0:T(1024)S(1)}, f32[1024]{0:T(1024)}, u32[]{:S(2)}) copy-start(f32[1024]{0:T(1024)} %param.14) | copy-start | bytes 12292
  110.5 26.1 %all-to-all-start = ((f32[4,128,8]{2,0,1:T(4,128)}), f32[4,128,8]{2,0,1:T(4,128)S(1)}, u32[]{:S(2)}, u32[]{:S(2)}) async-start(f32[4,128,8]{2,0,1:T(4,128)} %copy.64), calls=%async_computation | async-start | bytes 524288 | tf_op jit(solution)/shard_map/all_to_all | solution.py:155
  127.8 31.9 %collective-permute-start.2 = (f32[4,1,128,256]{3,2,1,0:T(8,128)}, f32[4,1,128,256]{3,2,1,0:T(8,128)S(1)}, u32[]{:S(2)}, u32[]{:S(2)}) collective-permute-start(f32[4,1,128,256]{3,2,1,0:T(8,128)} %get-tuple-element.24), channel_id=1, source_target_pairs={{1,0},{2,1},{3,2},{4,3},{5,4},{6,5},{7,6},{8,7},{9,8},{10,9},{11,1... | collective-permute-start | bytes 1572872 | tf_op jit(solution)/shard_map/ppermute | solution.py:27
  128.9 30.8 %collective-permute-start.3 = (f32[4,1,128,256]{3,2,1,0:T(8,128)}, f32[4,1,128,256]{3,2,1,0:T(8,128)}, u32[]{:S(2)}, u32[]{:S(2)}) collective-permute-start(f32[4,1,128,256]{3,2,1,0:T(8,128)} %get-tuple-element.23), channel_id=1, source_target_pairs={{0,1},{1,2},{2,3},{3,4},{4,5},{5,6},{6,7},{7,8},{8,9},{9,10},{10,1... | collective-permute-start | bytes 1572872 | tf_op jit(solution)/shard_map/ppermute | solution.py:25
  139.4 18.5 %all-to-all-start.1 = ((f32[4,128,8]{2,0,1:T(4,128)}), f32[4,128,8]{2,0,1:T(4,128)S(1)}, u32[]{:S(2)}, u32[]{:S(2)}) async-start(f32[4,128,8]{2,0,1:T(4,128)} %copy.69), calls=%async_computation.1 | async-start | bytes 524288 | tf_op jit(solution)/shard_map/all_to_all | solution.py:157
where the time goes:
time: 189 us; the launch traced here: 188 us
  other arithmetic  90.7 us (48%)
  local copies, waits for them, and re-layouts  54.4 us (29%)
  starting transfers between devices  26.8 us (14%)
  waiting for transfers between devices  12.7 us (7%)
  matrix products  2.73 us (1%)
    reduce_sum x1, other arithmetic, sample_lines(): along_line = jnp.sum(picked * depth_weights[None, None], axis=3)  30.1 us
    add x1, other arithmetic, on_device(): 0.5 * state + 0.5 * (middle + time_step * transport(with_rims(middle)))  28.5 us
    add x1, other arithmetic, on_device(): middle = state + time_step * transport(with_rims(state))  26.2 us
    gather x1, local copies, waits for them, and re-layouts, sample_lines(): picked = jnp.take(lines, line_ids, axis=1).reshape(4, 4, points, line_cells)  22.2 us
    all_to_all x1, starting transfers between devices, on_device(): lax.all_to_all(outgoing, 'blk', split_axis=1, concat_axis=1, tiled=True)  15 us
    add x1, local copies, waits for them, and re-layouts, on_device(): middle = state + time_step * transport(with_rims(state))  12.4 us
    mul x2, local copies, waits for them, and re-layouts, transport(): velocity[0] * (east_side - west_side)  11.1 us
    all_to_all x1, starting transfers between devices, on_device(): lax.all_to_all(solved, 'blk', split_axis=1, concat_axis=1, tiled=True)  7.38 us
  transfers between devices with their start and end apart: 6, of which 2 were waited for; matrix products, arithmetic and copies ran while one was open for 13% of the time, Pallas kernels for 0%

commit v1 on v0

v1 whole, which is shorter than its diff:
```python
import functools
import jax
import jax.numpy as jnp
from jax import lax
from jax.experimental import pallas as pl
from jax.experimental.pallas import tpu as pltpu
from jax.sharding import PartitionSpec as P

CX = 16
NY = 128
NZ = 256
POINTS = 512
NPTS = 64
NEWTON = 3
CAP = 8
COMPS = 4
LANES = 128
HALVES = NZ // LANES
PITCH = NY + 8
BLOCKS = HALVES * COMPS
LAYER = BLOCKS * PITCH
TILES = NY // 8
SHEET = BLOCKS * NY

time_step = 0.1
grid_viscosity = 0.2
karman = 0.41
prandtl = 0.72
turb_prandtl = 0.9
speed_floor = 0.5


def load8(flat, base, pitch):
    return [[flat[pl.ds(base + (h * COMPS + c) * pitch, 8), :] for c in range(COMPS)] for h in range(HALVES)]


def load8a(flat, base, pitch):
    return [
        [flat[pl.ds(pl.multiple_of(base + (h * COMPS + c) * pitch, 8), 8), :] for c in range(COMPS)]
        for h in range(HALVES)
    ]


def store8(flat, base, pitch, tiles):
    for h in range(HALVES):
        for c in range(COMPS):
            flat[pl.ds(pl.multiple_of(base + (h * COMPS + c) * pitch, 8), 8), :] = tiles[h][c]


def base_of(layer, yb):
    return layer * LAYER + yb * 8 + 8


def shifted(tiles):
    lane = lax.broadcasted_iota(jnp.int32, (8, LANES), 1)
    upper = [[None] * COMPS for _ in range(HALVES)]
    lower = [[None] * COMPS for _ in range(HALVES)]
    for c in range(COMPS):
        r0 = pltpu.roll(tiles[0][c], LANES - 1, 1)
        r1 = pltpu.roll(tiles[1][c], LANES - 1, 1)
        l0 = pltpu.roll(tiles[0][c], 1, 1)
        l1 = pltpu.roll(tiles[1][c], 1, 1)
        upper[0][c] = jnp.where(lane == LANES - 1, r1, r0)
        upper[1][c] = r1
        lower[0][c] = l0
        lower[1][c] = jnp.where(lane == 0, l0, l1)
    return upper, lower


def coefficients(center, scale):
    lane = lax.broadcasted_iota(jnp.int32, (8, LANES), 1)
    rest = grid_viscosity * scale
    coefs = []
    for h in range(HALVES):
        minus, plus = [], []
        for d in range(3):
            drift = center[h][d] * (0.5 * scale)
            minus.append(rest - drift)
            plus.append(rest + drift)
        coefs.append((minus, plus))
    coefs[1][0][2] = jnp.where(lane == LANES - 1, 0.0, coefs[1][0][2])
    coefs[0][1][2] = jnp.where(lane == 0, 0.0, coefs[0][1][2])
    return coefs


def blend(sides, h, c, coefs):
    minus, plus = coefs[h]
    (east, west), (north, south), (upper, lower) = sides
    xs = minus[0] * east[h][c] + plus[0] * west[h][c]
    ys = minus[1] * north[h][c] + plus[1] * south[h][c]
    zs = minus[2] * upper[h][c] + plus[2] * lower[h][c]
    return (xs + ys) + zs


def middle_tile(s, su, sl, x, yb, shift_base, shift_pitch):
    b = base_of(x, yb)
    center = load8a(s, b, PITCH)
    sides = (
        (load8a(s, b + LAYER, PITCH), load8a(s, b - LAYER, PITCH)),
        (load8(s, b + 1, PITCH), load8(s, b - 1, PITCH)),
        (load8a(su, shift_base, shift_pitch), load8a(sl, shift_base, shift_pitch)),
    )
    coefs = coefficients(center, time_step)
    keep = 1.0 - 6.0 * grid_viscosity * time_step
    return [[blend(sides, h, c, coefs) + keep * center[h][c] for c in range(COMPS)] for h in range(HALVES)]


def final_tile(s, s_layer, m, mu, ml, x, yb, shift_base, east=None):
    b = base_of(x, yb)
    center = load8a(m, b, PITCH)
    if east is None:
        east = load8a(m, b + LAYER, PITCH)
    sides = (
        (east, load8a(m, b - LAYER, PITCH)),
        (load8(m, b + 1, PITCH), load8(m, b - 1, PITCH)),
        (load8a(mu, shift_base, NY), load8a(ml, shift_base, NY)),
    )
    coefs = coefficients(center, 0.5 * time_step)
    keep = 0.5 - 3.0 * grid_viscosity * time_step
    old = load8a(s, base_of(s_layer, yb), PITCH)
    return [
        [blend(sides, h, c, coefs) + (keep * center[h][c] + 0.5 * old[h][c]) for c in range(COMPS)]
        for h in range(HALVES)
    ]


def zero_pads(ref, layers):
    def body(x, carry):
        for h in range(HALVES):
            for c in range(COMPS):
                ref[x, h, c, 0:8, :] = jnp.zeros((8, LANES), jnp.float32)
        return carry

    lax.fori_loop(0, layers, body, 0)


def half_layer(array, x, h):
    return array.at[:, x, :, pl.ds(h * LANES, LANES)]


def interior(state, final, mid, S, M, F, SU, SL, MU, ML, in_sem, mid_sem, out_sem):
    def in_copy(x, h):
        return pltpu.make_async_copy(half_layer(state, x, h), S.at[x, h, :, pl.ds(8, NY), :], in_sem.at[x, h])

    def mid_copy(x):
        return pltpu.make_async_copy(M.at[x], mid.at[x], mid_sem.at[x])

    def out_copy(x, h):
        return pltpu.make_async_copy(F.at[x & 1, h], half_layer(final, x, h), out_sem.at[x & 1, h])

    for x in range(CX):
        for h in range(HALVES):
            in_copy(x, h).start()
    zero_pads(S, CX + 1)
    zero_pads(M, CX + 1)
    s = S.reshape((CX + 1) * LAYER, LANES)
    m = M.reshape((CX + 1) * LAYER, LANES)
    f = F.reshape(2 * SHEET, LANES)

    def landed(x):
        for h in range(HALVES):
            in_copy(x, h).wait()

    landed(0)
    landed(1)
    for yb in range(TILES):
        u, l = shifted(load8a(s, base_of(1, yb), PITCH))
        store8(SU, yb * 64, 8, u)
        store8(SL, yb * 64, 8, l)

    def sweep(x, with_final):
        mids = [middle_tile(s, SU, SL, x, yb, yb * 64, 8) for yb in range(TILES)]
        if with_final:
            rb = ((x - 1) & 1) * SHEET
            fins = [
                final_tile(s, x - 1, m, MU, ML, x - 1, yb, rb + yb * 8, mids[yb]) for yb in range(TILES)
            ]
        news = [shifted(load8a(s, base_of(x + 1, yb), PITCH)) for yb in range(TILES)]
        for yb in range(TILES):
            store8(m, base_of(x, yb), PITCH, mids[yb])
            if with_final:
                store8(f, ((x - 1) & 1) * SHEET + yb * 8, NY, fins[yb])
            store8(SU, yb * 64, 8, news[yb][0])
            store8(SL, yb * 64, 8, news[yb][1])
            u, l = shifted(mids[yb])
            store8(MU, (x & 1) * SHEET + yb * 8, NY, u)
            store8(ML, (x & 1) * SHEET + yb * 8, NY, l)

    def head(x, carry):
        landed(x + 1)
        sweep(x, False)
        mid_copy(x).start()
        return carry

    lax.fori_loop(1, 3, head, 0)

    def main(x, carry):
        landed(x + 1)

        @pl.when(x >= 5)
        def _():
            for h in range(HALVES):
                out_copy(x - 3, h).wait()

        sweep(x, True)
        mid_copy(x).start()
        for h in range(HALVES):
            out_copy(x - 1, h).start()
        return carry

    lax.fori_loop(3, CX - 1, main, 0)

    def drain(x, carry):
        mid_copy(x).wait()
        return carry

    lax.fori_loop(1, CX - 1, drain, 0)
    for x in (CX - 4, CX - 3):
        for h in range(HALVES):
            out_copy(x, h).wait()


def run_interior(state):
    f32 = jnp.float32
    field = (CX + 1, HALVES, COMPS, PITCH, LANES)
    return pl.pallas_call(
        interior,
        out_shape=(
            jax.ShapeDtypeStruct((COMPS, CX, NY, NZ), f32),
            jax.ShapeDtypeStruct((CX, HALVES, COMPS, PITCH, LANES), f32),
        ),
        in_specs=[pl.BlockSpec(memory_space=pl.ANY)],
        out_specs=(pl.BlockSpec(memory_space=pl.ANY), pl.BlockSpec(memory_space=pl.ANY)),
        scratch_shapes=[
            pltpu.VMEM(field, f32),
            pltpu.VMEM(field, f32),
            pltpu.VMEM((2, HALVES, COMPS, NY, LANES), f32),
            pltpu.VMEM((SHEET, LANES), f32),
            pltpu.VMEM((SHEET, LANES), f32),
            pltpu.VMEM((2 * SHEET, LANES), f32),
            pltpu.VMEM((2 * SHEET, LANES), f32),
            pltpu.SemaphoreType.DMA((CX, 2)),
            pltpu.SemaphoreType.DMA((CX,)),
            pltpu.SemaphoreType.DMA((2, 2)),
        ],
        compiler_params=pltpu.CompilerParams(vmem_limit_bytes=56 << 20),
        name="interior",
    )(state)


def face_values(owner_row, received):
    owners = lax.broadcasted_iota(jnp.int32, (LANES, POINTS), 0)
    hit = owners == owner_row
    before = lax.broadcasted_iota(jnp.int32, (POINTS, POINTS), 0) < lax.broadcasted_iota(
        jnp.int32, (POINTS, POINTS), 1
    )
    earlier = jnp.dot(
        hit.astype(jnp.bfloat16), before.astype(jnp.bfloat16), preferred_element_type=jnp.float32
    )
    rank = jnp.sum(jnp.where(hit, earlier, 0.0), axis=0, keepdims=True)
    picked = jnp.dot(
        jnp.transpose(received),
        hit.astype(jnp.float32),
        precision=lax.Precision.HIGHEST,
        preferred_element_type=jnp.float32,
    )
    slot = lax.broadcasted_iota(jnp.int32, (CAP, POINTS), 0).astype(jnp.float32) == rank
    return [
        jnp.sum(jnp.where(slot, picked[CAP * v : CAP * v + CAP], 0.0), axis=0, keepdims=True) for v in range(5)
    ]


def wall_model(sample, theta, phi, height, wall_temp, viscosity):
    sin_theta = jnp.sin(theta)
    normal = [sin_theta * jnp.cos(phi), sin_theta * jnp.sin(phi), jnp.cos(theta)]
    normal_speed = sample[0] * normal[0] + sample[1] * normal[1] + sample[2] * normal[2]
    tangent = [sample[d] - normal_speed * normal[d] for d in range(3)]
    length = jnp.sqrt(tangent[0] * tangent[0] + tangent[1] * tangent[1] + tangent[2] * tangent[2])
    tangent_speed = jnp.maximum(length, speed_floor)
    ladder = (lax.broadcasted_iota(jnp.int32, (NPTS, POINTS), 0).astype(jnp.float32) + 0.5) / NPTS
    heights = height * (ladder * ladder)
    quad_weights = height * (ladder * (2.0 / NPTS))
    rise = karman * heights
    slope_weights = quad_weights * rise
    friction = jnp.sqrt(viscosity * tangent_speed / height)
    for newton_step in range(NEWTON):
        inverse = 1.0 / (viscosity + rise * friction)
        inverse_sum = jnp.sum(quad_weights * inverse, axis=0, keepdims=True)
        slope_sum = jnp.sum(slope_weights * (inverse * inverse), axis=0, keepdims=True)
        residual = friction * friction * inverse_sum - tangent_speed
        derivative = 2.0 * friction * inverse_sum - friction * friction * slope_sum
        friction = friction - residual / derivative
    conduct = viscosity / prandtl + rise * (friction / turb_prandtl)
    resist = jnp.sum(quad_weights / conduct, axis=0, keepdims=True)
    stress = friction * friction / tangent_speed
    return [stress * tangent[0], stress * tangent[1], stress * tangent[2], (sample[3] - wall_temp) / resist]


UNROLL = 32


def edges(
    cells, fracs, owner, received, state, mid, west_halo, east_halo, begun, final, flux,
    S, M, F, SU, SL, MU, ML, Q, in_sem, mid_sem, out_sem,
):
    sources = (
        (west_halo, 0), (west_halo, 1), (state, 0), (state, 1),
        (state, CX - 2), (state, CX - 1), (east_halo, 0), (east_halo, 1),
    )

    def in_copy(k, h):
        array, x = sources[k]
        return pltpu.make_async_copy(half_layer(array, x, h), S.at[k, h, :, pl.ds(8, NY), :], in_sem.at[k, h])

    def mid_copy(x):
        return pltpu.make_async_copy(mid.at[x], M.at[x + 1], mid_sem.at[x])

    for k in range(8):
        for h in range(HALVES):
            in_copy(k, h).start()
    for x in (1, 2, 13, 14):
        mid_copy(x).start()
    for x in range(3, 13):
        mid_copy(x).start()
    zero_pads(S, 9)
    for x in (0, 1, CX, CX + 1, CX + 2):
        for h in range(HALVES):
            for c in range(COMPS):
                M[x, h, c, 0:8, :] = jnp.zeros((8, LANES), jnp.float32)
    s = S.reshape(9 * LAYER, LANES)
    m = M.reshape((CX + 3) * LAYER, LANES)
    f = F.reshape(4 * SHEET, LANES)
    values = face_values(owner[...], received[...])
    for k in range(8):
        for h in range(HALVES):
            in_copy(k, h).wait()

    def s_layer(n):
        return 1 + (n & 1) + (n >> 1) * 4

    def m_layer(n):
        return (n & 1) + (n >> 1) * CX

    def roll_state(n, carry):
        for yb in range(TILES):
            u, l = shifted(load8a(s, base_of(s_layer(n), yb), PITCH))
            store8(SU, n * SHEET + yb * 8, NY, u)
            store8(SL, n * SHEET + yb * 8, NY, l)
        return carry

    lax.fori_loop(0, 4, roll_state, 0)

    def middle(n, carry):
        for yb in range(TILES):
            tile = middle_tile(s, SU, SL, s_layer(n), yb, n * SHEET + yb * 8, NY)
            store8(m, base_of(m_layer(n), yb), PITCH, tile)
        return carry

    lax.fori_loop(0, 4, middle, 0)
    for x in (1, 2, 13, 14):
        mid_copy(x).wait()

    def final_layer(n):
        return (n & 1) + (n >> 1) * (CX - 2)

    def roll_mid(n, carry):
        for yb in range(TILES):
            u, l = shifted(load8a(m, base_of(final_layer(n) + 1, yb), PITCH))
            store8(MU, n * SHEET + yb * 8, NY, u)
            store8(ML, n * SHEET + yb * 8, NY, l)
        return carry

    lax.fori_loop(0, 4, roll_mid, 0)

    def out_copy(n, h):
        return pltpu.make_async_copy(F.at[n, h], half_layer(final, final_layer(n), h), out_sem.at[n, h])

    def last(n, carry):
        for yb in range(TILES):
            tile = final_tile(s, 2 + n, m, MU, ML, final_layer(n) + 1, yb, n * SHEET + yb * 8)
            store8(f, n * SHEET + yb * 8, NY, tile)
        for h in range(HALVES):
            out_copy(n, h).start()
        return carry

    lax.fori_loop(0, 4, last, 0)
    for x in range(3, 13):
        mid_copy(x).wait()

    lane = lax.broadcasted_iota(jnp.int32, (8, LANES), 1)
    along = lane + LANES * (lax.broadcasted_iota(jnp.int32, (8, LANES), 0) // COMPS)

    def points(group, acc):
        total = acc
        first = group * UNROLL
        for p in range(UNROLL):
            e = first + p
            cell = cells[e]
            row = (lax.shift_right_logical(cell, 15) + 1) * LAYER + 8 + (lax.shift_right_logical(cell, 8) & (NY - 1))
            k = cell & (NZ - 1)
            fx, fy, fz = fracs[0, e], fracs[1, e], fracs[2, e]
            near0 = m[pl.ds(row, 8, stride=PITCH), :]
            near1 = m[pl.ds(row + 1, 8, stride=PITCH), :]
            far0 = m[pl.ds(row + LAYER, 8, stride=PITCH), :]
            far1 = m[pl.ds(row + LAYER + 1, 8, stride=PITCH), :]
            wide = (1.0 - fx) * ((1.0 - fy) * near0 + fy * near1) + fx * ((1.0 - fy) * far0 + fy * far1)
            depth = jnp.where(along == k, 1.0 - fz, jnp.where(along == k + 1, fz, 0.0))
            value = jnp.sum(wide * depth, axis=1, keepdims=True)
            total = jnp.where(lane == (e & (LANES - 1)), value, total)
        return total

    zero = jnp.zeros((8, LANES), jnp.float32)
    for q in range(POINTS // LANES):
        per = LANES // UNROLL
        got = lax.fori_loop(q * per, q * per + per, points, zero)
        Q[:, q * LANES : (q + 1) * LANES] = got
    both = Q[...]
    sampled = both[0:COMPS] + both[COMPS : 2 * COMPS]
    sample = [sampled[c : c + 1] for c in range(COMPS)]
    rows = wall_model(sample, *values)
    for c in range(COMPS):
        flux[c : c + 1, :] = rows[c]
    for n in range(4):
        for h in range(HALVES):
            out_copy(n, h).wait()


def run_edges(cells, fracs, owner, received, state, mid, west_halo, east_halo, begun):
    f32 = jnp.float32
    smem = pl.BlockSpec(memory_space=pltpu.SMEM)
    vmem = pl.BlockSpec(memory_space=pltpu.VMEM)
    hbm = pl.BlockSpec(memory_space=pl.ANY)
    return pl.pallas_call(
        edges,
        out_shape=(
            jax.ShapeDtypeStruct((COMPS, CX, NY, NZ), f32),
            jax.ShapeDtypeStruct((COMPS, POINTS), f32),
        ),
        in_specs=[smem, smem, vmem, vmem, hbm, hbm, hbm, hbm, hbm],
        out_specs=(hbm, vmem),
        input_output_aliases={8: 0},
        scratch_shapes=[
            pltpu.VMEM((9, HALVES, COMPS, PITCH, LANES), f32),
            pltpu.VMEM((CX + 3, HALVES, COMPS, PITCH, LANES), f32),
            pltpu.VMEM((4, HALVES, COMPS, NY, LANES), f32),
            pltpu.VMEM((4 * SHEET, LANES), f32),
            pltpu.VMEM((4 * SHEET, LANES), f32),
            pltpu.VMEM((4 * SHEET, LANES), f32),
            pltpu.VMEM((4 * SHEET, LANES), f32),
            pltpu.VMEM((8, POINTS), f32),
            pltpu.SemaphoreType.DMA((8, 2)),
            pltpu.SemaphoreType.DMA((CX,)),
            pltpu.SemaphoreType.DMA((4, 2)),
        ],
        compiler_params=pltpu.CompilerParams(vmem_limit_bytes=56 << 20),
        name="edges",
    )(cells, fracs, owner, received, state, mid, west_halo, east_halo, begun)


def on_device(
    state, sample_cell, sample_frac, sample_owner, face_angles, face_height, wall_temp, face_visc
):
    count = lax.axis_size("blk")
    ahead = [(i, (i + 1) % count) for i in range(count)]
    back = [((i + 1) % count, i) for i in range(count)]
    west_halo = lax.ppermute(state[:, CX - 2 :], "blk", ahead)
    east_halo = lax.ppermute(state[:, :2], "blk", back)
    faces = jnp.concatenate([face_angles, face_height[None], wall_temp[None], face_visc[None]], axis=0)
    faces = faces.reshape(5, count, CAP).transpose(1, 0, 2).reshape(count, 5 * CAP)
    faces = jnp.pad(faces, ((0, 0), (0, LANES - 5 * CAP)))
    received = lax.all_to_all(faces, "blk", split_axis=0, concat_axis=0, tiled=True)
    begun, mid = run_interior(state)
    owner = sample_owner.reshape(1, POINTS)
    return run_edges(sample_cell, sample_frac, owner, received, state, mid, west_halo, east_halo, begun)


def solution(mesh):
    placed = (
        P(None, "blk", None, None),
        P("blk"),
        P(None, "blk"),
        P("blk", None),
        P(None, "blk"),
        P("blk"),
        P("blk"),
        P("blk"),
    )
    return jax.shard_map(
        on_device,
        mesh=mesh,
        in_specs=placed,
        out_specs=(P(None, "blk", None, None), P(None, "blk")),
        check_vma=False,
    )
```

time: 189 us -> 57.9 us (0.31)
  other arithmetic: 90.7 us -> 0.01 us
  local copies, waits for them, and re-layouts: 54.4 us -> 8.21 us
  Pallas kernels: 0 us -> 30.9 us
  waiting for transfers between devices: 12.7 us -> 0.01 us
  starting transfers between devices: 26.8 us -> 17.7 us
  matrix products: 2.73 us -> 0 us
    add x6 -> x0, other arithmetic: 56.4 us -> none  [the longest x1 28.5 us: on_device(): 0.5 * state + 0.5 * (middle + time_step * transport(with_rims(middle)))]
    reduce_sum x9 -> x0, other arithmetic: 31.9 us -> none  [the longest x1 30.1 us: sample_lines(): along_line = jnp.sum(picked * depth_weights[None, None], axis=3)]
    pallas_call x0 -> x2, Pallas kernels: none -> 30.9 us  [the longest x1 15.7 us: run_interior(): pl.pallas_call(interior, out_shape=(jax.ShapeDtypeStruct((COMPS, CX, NY,...]
    gather x1 -> x0, local copies, waits for them, and re-layouts: 22.2 us -> none  [sample_lines(): picked = jnp.take(lines, line_ids, axis=1).reshape(4, 4, points, line_cells)]
    all_to_all x2 -> x1, waiting for transfers between devices: 12.6 us -> 0.01 us  [on_device(): lax.all_to_all(faces, 'blk', split_axis=0, concat_axis=0, tiled=True)]
    add x1 -> x0, local copies, waits for them, and re-layouts: 12.4 us -> none  [on_device(): middle = state + time_step * transport(with_rims(state))]
    mul x4 -> x0, local copies, waits for them, and re-layouts: 11.3 us -> none  [the longest x2 11.1 us: transport(): velocity[0] * (east_side - west_side)]
    all_to_all x2 -> x1, starting transfers between devices: 22.4 us -> 15 us  [on_device(): lax.all_to_all(faces, 'blk', split_axis=0, concat_axis=0, tiled=True)]
  transfers between devices with their start and end apart: 6 -> 3, of which waited for: 2 -> 0; matrix products, arithmetic and copies ran while one was open for 13% -> 7% of each run, Pallas kernels for 0% -> 27%
where the time goes in v1:
time: 57.9 us; the launch traced here: 57.5 us
  Pallas kernels  30.9 us (53%)
  starting transfers between devices  17.7 us (31%)
  local copies, waits for them, and re-layouts  8.21 us (14%)
  between operations  0.74 us (1%)
    pallas_call x1, Pallas kernels, run_interior(): pl.pallas_call(interior, out_shape=(jax.ShapeDtypeStruct((COMPS, CX, NY,...  15.7 us
    pallas_call x1, Pallas kernels, run_edges(): pl.pallas_call(edges, out_shape=(jax.ShapeDtypeStruct((COMPS, CX, NY, NZ)...  15.1 us
    all_to_all x1, starting transfers between devices, on_device(): lax.all_to_all(faces, 'blk', split_axis=0, concat_axis=0, tiled=True)  15 us
    concatenate x8, local copies, waits for them, and re-layouts, on_device(): jnp.concatenate([face_angles, face_height[None], wall_temp[None], face_vi...  3.36 us
    slice x1, local copies, waits for them, and re-layouts, on_device(): east_halo = lax.ppermute(state[:, :2], 'blk', back)  2.74 us
    ppermute x1, starting transfers between devices, on_device(): east_halo = lax.ppermute(state[:, :2], 'blk', back)  1.42 us
    unnamed x6, local copies, waits for them, and re-layouts  1.36 us
    ppermute x1, starting transfers between devices, on_device(): west_halo = lax.ppermute(state[:, CX - 2:], 'blk', ahead)  1.27 us
  transfers between devices with their start and end apart: 3, of which 0 were waited for; matrix products, arithmetic and copies ran while one was open for 7% of the time, Pallas kernels for 27%

profile of v1, /device:TPU:1, one launch (start us, length us, event | category | flops | bytes accessed | tf_op | source)
XLA Modules:
  0.0 57.5 jit_solution(7496173183274767382)
XLA Ops:
  0.6 2.7 %fusion = (f32[4,2,128,256]{3,2,1,0:T(8,128)}, f32[4,2,128,256]{3,2,1,0:T(8,128)S(1)}) fusion(f32[4,16,128,256]{3,2,1,0:T(8,128)} %state.3), kind=kLoop, calls=%fused_computation.2 | loop fusion | bytes 4194304 | tf_op jit(solution)/shard_map/slice | solution.py:467
  3.4 1.4 %collective-permute-start.1 = (f32[4,2,128,256]{3,2,1,0:T(8,128)}, f32[4,2,128,256]{3,2,1,0:T(8,128)S(1)}, u32[]{:S(2)}, u32[]{:S(2)}) collective-permute-start(f32[4,2,128,256]{3,2,1,0:T(8,128)} %get-tuple-element.6), channel_id=1, source_target_pairs={{1,0},{2,1},{3,2},{4,3},{5,4},{6,5},{7,6},{8,7},{9,8},{10,9},{11,1... | collective-permute-start | bytes 3145736 | tf_op jit(solution)/shard_map/ppermute | solution.py:467
  4.8 1.3 %collective-permute-start = (f32[4,2,128,256]{3,2,1,0:T(8,128)S(1)}, f32[4,2,128,256]{3,2,1,0:T(8,128)S(1)}, u32[]{:S(2)}, u32[]{:S(2)}) collective-permute-start(f32[4,2,128,256]{3,2,1,0:T(8,128)S(1)} %get-tuple-element.7), channel_id=1, source_target_pairs={{0,1},{1,2},{2,3},{3,4},{4,5},{5,6},{6,7},{7,8},{8,9},{9,10},{10,1... | collective-permute-start | bytes 3145736 | tf_op jit(solution)/shard_map/ppermute | solution.py:466
  6.1 0.8 %concatenate.13 = f32[1,128,8]{2,1,0:T(8,128)S(1)} reshape(f32[1024]{0:T(1024)} %param.13) | data formatting | bytes 8192 | tf_op jit(solution)/shard_map/concatenate | solution.py:468
  6.9 0.8 %concatenate.14 = f32[1,128,8]{2,1,0:T(8,128)S(1)} reshape(f32[1024]{0:T(1024)} %param.14) | data formatting | bytes 8192 | tf_op jit(solution)/shard_map/concatenate | solution.py:468
  7.7 0.8 %concatenate.15 = f32[1,128,8]{2,1,0:T(8,128)S(1)} reshape(f32[1024]{0:T(1024)} %param.15) | data formatting | bytes 8192 | tf_op jit(solution)/shard_map/concatenate | solution.py:468
  8.6 0.8 %concatenate.12 = f32[2,128,8]{2,1,0:T(8,128)S(1)} reshape(f32[2,1024]{1,0:T(2,128)} %param.12) | data formatting | bytes 16384 | tf_op jit(solution)/shard_map/concatenate | solution.py:468
  9.4 0.1 copy.14
  9.5 0.7 %copy.18 = f32[128,1,128]{2,1,0:T(1,128)} copy(f32[128,1,128]{0,2,1:T(8,128)S(1)} %pad_bitcast_fusion) | data formatting | bytes 131072 | tf_op jit(solution)/shard_map/all_to_all | solution.py:471
  10.2 15.0 %all-to-all-start = ((f32[128,1,128]{2,1,0:T(1,128)}), f32[128,1,128]{2,1,0:T(1,128)S(1)}, u32[]{:S(2)}, u32[]{:S(2)}) async-start(f32[128,1,128]{2,1,0:T(1,128)} %copy.18), calls=%async_computation | async-start | bytes 131072 | tf_op jit(solution)/shard_map/all_to_all | solution.py:471
  25.2 15.7 %interior.1 = (f32[4,16,128,256]{3,2,1,0:T(8,128)}, f32[16,2,4,136,128]{4,3,2,1,0:T(8,128)}) custom-call(f32[4,16,128,256]{3,2,1,0:T(8,128)} %state.3), custom_call_target="tpu_custom_call" | custom-call | tf_op jit(solution)/shard_map/interior/pallas_call | solution.py:226
  40.9 0.0 all-to-all-done
  41.0 0.0 copy-start.2
  41.0 0.0 collective-permute-done.1.east_halo
  41.0 0.0 copy-start
  41.0 0.0 collective-permute-done.west_halo
  41.0 0.0 copy-start.1
  41.0 0.6 copy-done.2
  41.6 0.4 copy-done
  42.0 0.4 copy-done.1
  42.4 15.1 %edges.1 = (f32[4,16,128,256]{3,2,1,0:T(8,128)}, f32[4,512]{1,0:T(4,128)}) custom-call(s32[512]{0:T(512)} %cells.1, f32[3,512]{1,0:T(4,128)} %fracs.1, s32[1,512]{1,0:T(1,128)} %bitcast.9, f32[128,128]{1,0:T(8,128)} %bitcast.8, f32[4,16,128,256]{3,2,1,0:T(8,128)} %state.3, ...), custom_call_target="tpu_custom_call", output_to_operand_aliasing={{0}: (8, {})} | custom-call | tf_op jit(solution)/shard_map/edges/pallas_call | solution.py:433
  (5 shorter events, 0.2 us)
Async XLA Ops:
  3.4 37.6 %collective-permute-start.1 = (f32[4,2,128,256]{3,2,1,0:T(8,128)}, f32[4,2,128,256]{3,2,1,0:T(8,128)S(1)}, u32[]{:S(2)}, u32[]{:S(2)}) collective-permute-start(f32[4,2,128,256]{3,2,1,0:T(8,128)} %get-tuple-element.6), channel_id=1, source_target_pairs={{1,0},{2,1},{3,2},{4,3},{5,4},{6,5},{7,6},{8,7},{9,8},{10,9},{11,1... | collective-permute-start | bytes 3145736 | tf_op jit(solution)/shard_map/ppermute | solution.py:467
  4.8 36.2 %collective-permute-start = (f32[4,2,128,256]{3,2,1,0:T(8,128)S(1)}, f32[4,2,128,256]{3,2,1,0:T(8,128)S(1)}, u32[]{:S(2)}, u32[]{:S(2)}) collective-permute-start(f32[4,2,128,256]{3,2,1,0:T(8,128)S(1)} %get-tuple-element.7), channel_id=1, source_target_pairs={{0,1},{1,2},{2,3},{3,4},{4,5},{5,6},{6,7},{7,8},{8,9},{9,10},{10,1... | collective-permute-start | bytes 3145736 | tf_op jit(solution)/shard_map/ppermute | solution.py:466
  10.2 30.7 %all-to-all-start = ((f32[128,1,128]{2,1,0:T(1,128)}), f32[128,1,128]{2,1,0:T(1,128)S(1)}, u32[]{:S(2)}, u32[]{:S(2)}) async-start(f32[128,1,128]{2,1,0:T(1,128)} %copy.18), calls=%async_computation | async-start | bytes 131072 | tf_op jit(solution)/shard_map/all_to_all | solution.py:471
  41.0 0.6 %copy-start.2 = (f32[128,1,128]{2,1,0:T(1,128)}, f32[128,1,128]{2,1,0:T(1,128)S(1)}, u32[]{:S(2)}) copy-start(f32[128,1,128]{2,1,0:T(1,128)S(1)} %all-to-all-done) | copy-start | bytes 196612
  41.0 1.0 %copy-start = (f32[4,2,128,256]{3,2,1,0:T(8,128)}, f32[4,2,128,256]{3,2,1,0:T(8,128)S(1)}, u32[]{:S(2)}) copy-start(f32[4,2,128,256]{3,2,1,0:T(8,128)S(1)} %collective-permute-done.1.east_halo) | copy-start | bytes 3145732
  41.0 1.4 %copy-start.1 = (f32[4,2,128,256]{3,2,1,0:T(8,128)}, f32[4,2,128,256]{3,2,1,0:T(8,128)S(1)}, u32[]{:S(2)}) copy-start(f32[4,2,128,256]{3,2,1,0:T(8,128)S(1)} %collective-permute-done.west_halo) | copy-start | bytes 3145732

commit v2 on v1

v2 whole, which is shorter than its diff:
```python
import functools
import jax
import jax.numpy as jnp
from jax import lax
from jax.experimental import pallas as pl
from jax.experimental.pallas import tpu as pltpu
from jax.sharding import PartitionSpec as P

CX = 16
NY = 128
NZ = 256
POINTS = 512
NPTS = 64
NEWTON = 3
CAP = 8
COMPS = 4
LANES = 128
HALVES = NZ // LANES
PITCH = NY + 8
BLOCKS = HALVES * COMPS
LAYER = BLOCKS * PITCH
TILES = NY // 8
SHEET = BLOCKS * NY

time_step = 0.1
grid_viscosity = 0.2
karman = 0.41
prandtl = 0.72
turb_prandtl = 0.9
speed_floor = 0.5


def load8(flat, base, pitch):
    return [[flat[pl.ds(base + (h * COMPS + c) * pitch, 8), :] for c in range(COMPS)] for h in range(HALVES)]


def load8a(flat, base, pitch):
    return [
        [flat[pl.ds(pl.multiple_of(base + (h * COMPS + c) * pitch, 8), 8), :] for c in range(COMPS)]
        for h in range(HALVES)
    ]


def store8(flat, base, pitch, tiles):
    for h in range(HALVES):
        for c in range(COMPS):
            flat[pl.ds(pl.multiple_of(base + (h * COMPS + c) * pitch, 8), 8), :] = tiles[h][c]


def base_of(layer, yb):
    return layer * LAYER + yb * 8 + 8


def shifted(tiles):
    lane = lax.broadcasted_iota(jnp.int32, (8, LANES), 1)
    upper = [[None] * COMPS for _ in range(HALVES)]
    lower = [[None] * COMPS for _ in range(HALVES)]
    for c in range(COMPS):
        r0 = pltpu.roll(tiles[0][c], LANES - 1, 1)
        r1 = pltpu.roll(tiles[1][c], LANES - 1, 1)
        l0 = pltpu.roll(tiles[0][c], 1, 1)
        l1 = pltpu.roll(tiles[1][c], 1, 1)
        upper[0][c] = jnp.where(lane == LANES - 1, r1, r0)
        upper[1][c] = r1
        lower[0][c] = l0
        lower[1][c] = jnp.where(lane == 0, l0, l1)
    return upper, lower


def coefficients(center, scale):
    lane = lax.broadcasted_iota(jnp.int32, (8, LANES), 1)
    rest = grid_viscosity * scale
    coefs = []
    for h in range(HALVES):
        minus, plus = [], []
        for d in range(3):
            drift = center[h][d] * (0.5 * scale)
            minus.append(rest - drift)
            plus.append(rest + drift)
        coefs.append((minus, plus))
    coefs[1][0][2] = jnp.where(lane == LANES - 1, 0.0, coefs[1][0][2])
    coefs[0][1][2] = jnp.where(lane == 0, 0.0, coefs[0][1][2])
    return coefs


def blend(sides, h, c, coefs):
    minus, plus = coefs[h]
    (east, west), (north, south), (upper, lower) = sides
    xs = minus[0] * east[h][c] + plus[0] * west[h][c]
    ys = minus[1] * north[h][c] + plus[1] * south[h][c]
    zs = minus[2] * upper[h][c] + plus[2] * lower[h][c]
    return (xs + ys) + zs


def middle_tile(s, m, su, sl, x, yb):
    b = base_of(x + 2, yb)
    center = load8a(s, b, PITCH)
    sides = (
        (load8a(s, b + LAYER, PITCH), load8a(s, b - LAYER, PITCH)),
        (load8(s, b + 1, PITCH), load8(s, b - 1, PITCH)),
        (load8a(su, yb * 8, NY), load8a(sl, yb * 8, NY)),
    )
    coefs = coefficients(center, time_step)
    keep = 1.0 - 6.0 * grid_viscosity * time_step
    tiles = [[blend(sides, h, c, coefs) + keep * center[h][c] for c in range(COMPS)] for h in range(HALVES)]
    store8(m, base_of(x + 1, yb), PITCH, tiles)


def final_tile(s, m, f, f_base, mu, ml, x, yb):
    b = base_of(x + 1, yb)
    center = load8a(m, b, PITCH)
    sides = (
        (load8a(m, b + LAYER, PITCH), load8a(m, b - LAYER, PITCH)),
        (load8(m, b + 1, PITCH), load8(m, b - 1, PITCH)),
        (load8a(mu, yb * 8, NY), load8a(ml, yb * 8, NY)),
    )
    coefs = coefficients(center, 0.5 * time_step)
    keep = 0.5 - 3.0 * grid_viscosity * time_step
    old = load8a(s, base_of(x + 2, yb), PITCH)
    tiles = [
        [blend(sides, h, c, coefs) + (keep * center[h][c] + 0.5 * old[h][c]) for c in range(COMPS)]
        for h in range(HALVES)
    ]
    store8(f, f_base + yb * 8, NY, tiles)


def roll_tile(field, layer, yb, u_ref, l_ref):
    u, l = shifted(load8a(field, base_of(layer, yb), PITCH))
    store8(u_ref, yb * 8, NY, u)
    store8(l_ref, yb * 8, NY, l)


def zero_pads(ref, layers):
    def body(x, carry):
        for h in range(HALVES):
            for c in range(COMPS):
                ref[x, h, c, 0:8, :] = jnp.zeros((8, LANES), jnp.float32)
        return carry

    lax.fori_loop(0, layers, body, 0)


def half_layer(array, x, h):
    return array.at[:, x, :, pl.ds(h * LANES, LANES)]


S_SHAPE = (CX + 5, HALVES, COMPS, PITCH, LANES)
M_SHAPE = (CX + 3, HALVES, COMPS, PITCH, LANES)
RIM_SHAPE = (COMPS, 2, NY, NZ)
LAG = 3

hbm_spec = pl.BlockSpec(memory_space=pl.ANY)
vmem_spec = pl.BlockSpec(memory_space=pltpu.VMEM)
smem_spec = pl.BlockSpec(memory_space=pltpu.SMEM)
sheet = pltpu.VMEM((SHEET, LANES), jnp.float32)


def in_hbm(x):
    return pltpu.with_memory_space_constraint(x, pltpu.HBM)


def on_chip(x):
    return pltpu.with_memory_space_constraint(x, pltpu.VMEM)


def packed_faces(rows):
    lane = lax.broadcasted_iota(jnp.int32, (LANES, LANES), 1)
    sub = lax.broadcasted_iota(jnp.int32, (LANES, LANES), 0)
    per = LANES // CAP
    mine = lax.shift_right_logical(lane, 3) == (sub & (per - 1))
    left, right = [], []
    for v, row in enumerate(rows):
        spread = jnp.concatenate(
            [jnp.broadcast_to(row[:, q * LANES : (q + 1) * LANES], (per, LANES)) for q in range(CAP)], axis=0
        )
        left.append(jnp.where(mine, spread, 0.0))
        right.append(((sub & (CAP - 1)) + v * CAP == lane).astype(jnp.float32))
    return jnp.dot(
        jnp.concatenate(left, axis=1),
        jnp.concatenate(right, axis=0),
        precision=lax.Precision.HIGHEST,
        preferred_element_type=jnp.float32,
    )


def opening(state, angles, height, temp, visc, to_west, to_east, packed, rim_sem):
    def rim_copy(k, c):
        if k == 0:
            return pltpu.make_async_copy(state.at[c, pl.ds(0, 2)], to_west.at[c], rim_sem.at[0, c])
        return pltpu.make_async_copy(state.at[c, pl.ds(CX - 2, 2)], to_east.at[c], rim_sem.at[1, c])

    for k in range(2):
        for c in range(COMPS):
            rim_copy(k, c).start()
    packed[...] = packed_faces([angles[0:1, :], angles[1:2, :], height[...], temp[...], visc[...]])
    for k in range(2):
        for c in range(COMPS):
            rim_copy(k, c).wait()


def run_opening(state, angles, height, temp, visc):
    f32 = jnp.float32
    return pl.pallas_call(
        opening,
        out_shape=(
            pltpu.VMEM(RIM_SHAPE, f32),
            pltpu.VMEM(RIM_SHAPE, f32),
            jax.ShapeDtypeStruct((LANES, LANES), f32),
        ),
        in_specs=[hbm_spec, vmem_spec, vmem_spec, vmem_spec, vmem_spec],
        out_specs=(vmem_spec, vmem_spec, vmem_spec),
        scratch_shapes=[pltpu.SemaphoreType.DMA((2, COMPS))],
        name="opening",
    )(in_hbm(state), angles, height, temp, visc)


def interior(
    state, S, M, final, F, SU0, SL0, SU1, SL1, MU0, ML0, MU1, ML1, in_sem, out_sem
):
    def in_copy(x, h):
        return pltpu.make_async_copy(half_layer(state, x, h), S.at[x + 2, h, :, pl.ds(8, NY), :], in_sem.at[x, h])

    def out_copy(y, h):
        return pltpu.make_async_copy(F.at[y - 2, h], half_layer(final, y, h), out_sem.at[y - 2, h])

    for x in range(CX):
        for h in range(HALVES):
            in_copy(x, h).start()
    zero_pads(S, CX + 5)
    zero_pads(M, CX + 3)
    s = S.reshape((CX + 5) * LAYER, LANES)
    m = M.reshape((CX + 3) * LAYER, LANES)
    f = F.reshape((CX - 4) * SHEET, LANES)
    state_rolled = ((SU0, SL0), (SU1, SL1))
    mid_rolled = ((MU0, ML0), (MU1, ML1))

    def landed(x):
        for h in range(HALVES):
            in_copy(x, h).wait()

    landed(0)
    landed(1)
    for yb in range(TILES):
        roll_tile(s, 3, yb, *state_rolled[1])

    def step(x, y, odd_x, odd_y, next_mid=None):
        for yb in range(TILES):
            if y is not None:
                final_tile(s, m, f, (y - 2) * SHEET, *mid_rolled[odd_y], y, yb)
            if next_mid is not None:
                roll_tile(m, next_mid + 1, yb, *mid_rolled[0 if y is None else 1 - odd_y])
        for yb in range(TILES):
            if x is not None:
                middle_tile(s, m, *state_rolled[odd_x], x, yb)
                roll_tile(s, x + 3, yb, *state_rolled[1 - odd_x])
        if y is not None:
            for h in range(HALVES):
                out_copy(y, h).start()

    landed(2)
    step(1, None, 1, 0)
    landed(3)
    step(2, None, 0, 0)
    landed(4)
    step(3, None, 1, 0)
    landed(5)
    step(4, None, 0, 0, next_mid=2)

    def both(p, carry):
        x = 5 + 2 * p
        y = x - LAG
        landed(x + 1)
        step(x, y, 1, 0, next_mid=y + 1)
        landed(x + 2)
        step(x + 1, y + 1, 0, 1, next_mid=y + 2)
        return carry

    lax.fori_loop(0, (CX - 6) // 2, both, 0)
    step(None, CX - 4, 0, 0, next_mid=CX - 3)
    step(None, CX - 3, 0, 1)
    for y in range(2, CX - 2):
        for h in range(HALVES):
            out_copy(y, h).wait()


def run_interior(state):
    f32 = jnp.float32
    return pl.pallas_call(
        interior,
        out_shape=(
            pltpu.VMEM(S_SHAPE, f32),
            pltpu.VMEM(M_SHAPE, f32),
            jax.ShapeDtypeStruct((COMPS, CX, NY, NZ), f32),
        ),
        in_specs=[hbm_spec],
        out_specs=(vmem_spec, vmem_spec, hbm_spec),
        scratch_shapes=[pltpu.VMEM((CX - 4, HALVES, COMPS, NY, LANES), f32)]
        + [sheet] * 8
        + [pltpu.SemaphoreType.DMA((CX, 2)), pltpu.SemaphoreType.DMA((CX - 4, 2))],
        compiler_params=pltpu.CompilerParams(vmem_limit_bytes=14 << 20),
        name="interior",
    )(in_hbm(state))


def edges(
    cells, fracs, S_in, M_in, west_halo, east_halo, begun, S, M, final, sampled,
    F, SU0, SL0, SU1, SL1, MU, ML, in_sem, out_sem,
):
    def in_copy(k, h):
        array = west_halo if k < 2 else east_halo
        layer = k if k < 2 else CX + k
        return pltpu.make_async_copy(
            half_layer(array, k & 1, h), S.at[layer, h, :, pl.ds(8, NY), :], in_sem.at[k, h]
        )

    for k in range(4):
        for h in range(HALVES):
            in_copy(k, h).start()
    s = S.reshape((CX + 5) * LAYER, LANES)
    m = M.reshape((CX + 3) * LAYER, LANES)
    f = F.reshape(4 * SHEET, LANES)
    rolled = ((SU0, SL0), (SU1, SL1))

    def mid_refs(n):
        return MU.at[pl.ds(n * SHEET, SHEET)], ML.at[pl.ds(n * SHEET, SHEET)]

    for yb in range(TILES):
        roll_tile(s, 2, yb, *rolled[0])
        roll_tile(m, 2, yb, *mid_refs(1))
    for k in range(4):
        for h in range(HALVES):
            in_copy(k, h).wait()
    for yb in range(TILES):
        middle_tile(s, m, *rolled[0], 0, yb)
        roll_tile(s, CX + 1, yb, *rolled[1])
        roll_tile(m, CX - 1, yb, *mid_refs(2))
    for yb in range(TILES):
        middle_tile(s, m, *rolled[1], CX - 1, yb)
        roll_tile(s, 1, yb, *rolled[0])
        roll_tile(m, 1, yb, *mid_refs(0))
    for yb in range(TILES):
        middle_tile(s, m, *rolled[0], -1, yb)
        roll_tile(s, CX + 2, yb, *rolled[1])
        roll_tile(m, CX, yb, *mid_refs(3))
    for yb in range(TILES):
        middle_tile(s, m, *rolled[1], CX, yb)

    def final_layer(n):
        return (n & 1) + (n >> 1) * (CX - 2)

    def out_copy(n, h):
        return pltpu.make_async_copy(F.at[n, h], half_layer(final, final_layer(n), h), out_sem.at[n, h])

    lane = lax.broadcasted_iota(jnp.int32, (8, LANES), 1)
    along = lane + LANES * (lax.broadcasted_iota(jnp.int32, (8, LANES), 0) // COMPS)

    def sampled_at(e):
        cell = cells[e]
        row = (lax.shift_right_logical(cell, 15) + 1) * LAYER + 8 + (lax.shift_right_logical(cell, 8) & (NY - 1))
        k = cell & (NZ - 1)
        fx, fy, fz = fracs[0, e], fracs[1, e], fracs[2, e]
        near0 = m[pl.ds(row, 8, stride=PITCH), :]
        near1 = m[pl.ds(row + 1, 8, stride=PITCH), :]
        far0 = m[pl.ds(row + LAYER, 8, stride=PITCH), :]
        far1 = m[pl.ds(row + LAYER + 1, 8, stride=PITCH), :]
        wide = (1.0 - fx) * ((1.0 - fy) * near0 + fy * near1) + fx * ((1.0 - fy) * far0 + fy * far1)
        depth = jnp.where(along == k, 1.0 - fz, jnp.where(along == k + 1, fz, 0.0))
        return jnp.sum(wide * depth, axis=1, keepdims=True)

    def last(n, carry):
        total = jnp.zeros((8, LANES), jnp.float32)
        per = LANES // TILES
        for yb in range(TILES):
            final_tile(s, m, f, n * SHEET, *mid_refs(n), final_layer(n), yb)
            for p in range(yb * per, yb * per + per):
                total = jnp.where(lane == p, sampled_at(n * LANES + p), total)
        sampled[n] = total
        for h in range(HALVES):
            out_copy(n, h).start()
        return carry

    lax.fori_loop(0, 4, last, 0)
    for n in range(4):
        for h in range(HALVES):
            out_copy(n, h).wait()


def run_edges(cells, fracs, S, M, west_halo, east_halo, begun):
    f32 = jnp.float32
    outs = pl.pallas_call(
        edges,
        out_shape=(
            pltpu.VMEM(S_SHAPE, f32),
            pltpu.VMEM(M_SHAPE, f32),
            jax.ShapeDtypeStruct((COMPS, CX, NY, NZ), f32),
            pltpu.VMEM((POINTS // LANES, 8, LANES), f32),
        ),
        in_specs=[smem_spec, smem_spec, vmem_spec, vmem_spec, vmem_spec, vmem_spec, hbm_spec],
        out_specs=(vmem_spec, vmem_spec, hbm_spec, vmem_spec),
        input_output_aliases={2: 0, 3: 1, 6: 2},
        scratch_shapes=[pltpu.VMEM((4, HALVES, COMPS, NY, LANES), f32)]
        + [sheet] * 4
        + [
            pltpu.VMEM((4 * SHEET, LANES), f32),
            pltpu.VMEM((4 * SHEET, LANES), f32),
            pltpu.SemaphoreType.DMA((4, 2)),
            pltpu.SemaphoreType.DMA((4, 2)),
        ],
        compiler_params=pltpu.CompilerParams(vmem_limit_bytes=14 << 20),
        name="edges",
    )(cells, fracs, on_chip(S), on_chip(M), on_chip(west_halo), on_chip(east_halo), begun)
    return outs[2], outs[3]


def face_values(owner_row, received):
    owners = lax.broadcasted_iota(jnp.int32, (LANES, POINTS), 0)
    hit = owners == owner_row
    before = lax.broadcasted_iota(jnp.int32, (POINTS, POINTS), 0) < lax.broadcasted_iota(
        jnp.int32, (POINTS, POINTS), 1
    )
    earlier = jnp.dot(
        hit.astype(jnp.bfloat16), before.astype(jnp.bfloat16), preferred_element_type=jnp.float32
    )
    rank = jnp.sum(jnp.where(hit, earlier, 0.0), axis=0, keepdims=True)
    picked = jnp.dot(
        jnp.transpose(received),
        hit.astype(jnp.float32),
        precision=lax.Precision.HIGHEST,
        preferred_element_type=jnp.float32,
    )
    slot = lax.broadcasted_iota(jnp.int32, (CAP, POINTS), 0).astype(jnp.float32) == rank
    return [
        jnp.sum(jnp.where(slot, picked[CAP * v : CAP * v + CAP], 0.0), axis=0, keepdims=True) for v in range(5)
    ]


def wall_model(sample, theta, phi, height, wall_temp, viscosity):
    sin_theta = jnp.sin(theta)
    normal = [sin_theta * jnp.cos(phi), sin_theta * jnp.sin(phi), jnp.cos(theta)]
    normal_speed = sample[0] * normal[0] + sample[1] * normal[1] + sample[2] * normal[2]
    tangent = [sample[d] - normal_speed * normal[d] for d in range(3)]
    length = jnp.sqrt(tangent[0] * tangent[0] + tangent[1] * tangent[1] + tangent[2] * tangent[2])
    tangent_speed = jnp.maximum(length, speed_floor)
    ladder = (lax.broadcasted_iota(jnp.int32, (NPTS, POINTS), 0).astype(jnp.float32) + 0.5) / NPTS
    heights = height * (ladder * ladder)
    quad_weights = height * (ladder * (2.0 / NPTS))
    rise = karman * heights
    slope_weights = quad_weights * rise
    friction = jnp.sqrt(viscosity * tangent_speed / height)
    for newton_step in range(NEWTON):
        inverse = 1.0 / (viscosity + rise * friction)
        inverse_sum = jnp.sum(quad_weights * inverse, axis=0, keepdims=True)
        slope_sum = jnp.sum(slope_weights * (inverse * inverse), axis=0, keepdims=True)
        residual = friction * friction * inverse_sum - tangent_speed
        derivative = 2.0 * friction * inverse_sum - friction * friction * slope_sum
        friction = friction - residual / derivative
    conduct = viscosity / prandtl + rise * (friction / turb_prandtl)
    resist = jnp.sum(quad_weights / conduct, axis=0, keepdims=True)
    stress = friction * friction / tangent_speed
    return [stress * tangent[0], stress * tangent[1], stress * tangent[2], (sample[3] - wall_temp) / resist]


def walls(owner, received, sampled, flux):
    values = face_values(owner[...], received[...])
    both = jnp.concatenate([sampled[n] for n in range(POINTS // LANES)], axis=1)
    total = both[0:COMPS] + both[COMPS : 2 * COMPS]
    rows = wall_model([total[c : c + 1] for c in range(COMPS)], *values)
    for c in range(COMPS):
        flux[c : c + 1, :] = rows[c]


def run_walls(owner, received, sampled):
    return pl.pallas_call(
        walls,
        out_shape=jax.ShapeDtypeStruct((COMPS, POINTS), jnp.float32),
        in_specs=[vmem_spec] * 3,
        out_specs=vmem_spec,
        name="walls",
    )(owner, on_chip(received), on_chip(sampled))


def on_device(
    state, sample_cell, sample_frac, sample_owner, face_angles, face_height, wall_temp, face_visc
):
    count = lax.axis_size("blk")
    ahead = [(i, (i + 1) % count) for i in range(count)]
    back = [((i + 1) % count, i) for i in range(count)]
    to_west, to_east, packed = run_opening(
        state, face_angles, face_height.reshape(1, -1), wall_temp.reshape(1, -1), face_visc.reshape(1, -1)
    )
    west_halo = lax.ppermute(to_east, "blk", ahead)
    east_halo = lax.ppermute(to_west, "blk", back)
    received = lax.all_to_all(packed, "blk", split_axis=0, concat_axis=0, tiled=True)
    S, M, begun = run_interior(state)
    final, sampled = run_edges(sample_cell, sample_frac, S, M, west_halo, east_halo, begun)
    return final, run_walls(sample_owner.reshape(1, POINTS), received, sampled)


def solution(mesh):
    placed = (
        P(None, "blk", None, None),
        P("blk"),
        P(None, "blk"),
        P("blk", None),
        P(None, "blk"),
        P("blk"),
        P("blk"),
        P("blk"),
    )
    return jax.shard_map(
        on_device,
        mesh=mesh,
        in_specs=placed,
        out_specs=(P(None, "blk", None, None), P(None, "blk")),
        check_vma=False,
    )
```

time: 57.9 us -> 47.4 us (0.82)
  local copies, waits for them, and re-layouts: 8.21 us -> 0.01 us
  starting transfers between devices: 17.7 us -> 13.3 us
  Pallas kernels: 30.9 us -> 33.1 us
    all_to_all x1, starting transfers between devices: 15 us -> 10.6 us  [on_device(): lax.all_to_all(packed, 'blk', split_axis=0, concat_axis=0, tiled=True)]
    concatenate x8 -> x0, local copies, waits for them, and re-layouts: 3.36 us -> none  [on_device(): jnp.concatenate([face_angles, face_height[None], wall_temp[None], face_vi...]
    slice x1 -> x0, local copies, waits for them, and re-layouts: 2.74 us -> none  [on_device(): east_halo = lax.ppermute(state[:, :2], 'blk', back)]
    pallas_call x2 -> x4, Pallas kernels: 30.9 us -> 33.1 us  [the longest x1 18 us: run_interior(): pl.pallas_call(interior, out_shape=(pltpu.VMEM(S_SHAPE, f32), pltpu.VMEM(...]
    unnamed x6 -> x4, local copies, waits for them, and re-layouts: 1.36 us -> 0.01 us
    all_to_all x2 -> x0, local copies, waits for them, and re-layouts: 0.74 us -> none  [on_device(): lax.all_to_all(faces, 'blk', split_axis=0, concat_axis=0, tiled=True)]
  transfers between devices with their start and end apart: 3 -> 3, of which waited for: 0 -> 0; matrix products, arithmetic and copies ran while one was open for 7% -> 0% of each run, Pallas kernels for 27% -> 59%
where the time goes in v2:
time: 47.4 us; the launch traced here: 47.2 us
  Pallas kernels  33.1 us (70%)
  starting transfers between devices  13.3 us (28%)
  between operations  0.72 us (2%)
    pallas_call x1, Pallas kernels, run_interior(): pl.pallas_call(interior, out_shape=(pltpu.VMEM(S_SHAPE, f32), pltpu.VMEM(...  18 us
    all_to_all x1, starting transfers between devices, on_device(): lax.all_to_all(packed, 'blk', split_axis=0, concat_axis=0, tiled=True)  10.6 us
    pallas_call x1, Pallas kernels, run_edges(): pl.pallas_call(edges, out_shape=(pltpu.VMEM(S_SHAPE, f32), pltpu.VMEM(M_S...  9.76 us
    pallas_call x1, Pallas kernels, run_opening(): pl.pallas_call(opening, out_shape=(pltpu.VMEM(RIM_SHAPE, f32), pltpu.VMEM...  3.32 us
    ppermute x1, starting transfers between devices, on_device(): west_halo = lax.ppermute(to_east, 'blk', ahead)  2.76 us
    pallas_call x1, Pallas kernels, run_walls(): pl.pallas_call(walls, out_shape=jax.ShapeDtypeStruct((COMPS, POINTS), jnp...  2.12 us
  transfers between devices with their start and end apart: 3, of which 0 were waited for; matrix products, arithmetic and copies ran while one was open for 0% of the time, Pallas kernels for 59%

profile of v2, /device:TPU:1, one launch (start us, length us, event | category | flops | bytes accessed | tf_op | source)
XLA Modules:
  0.0 47.2 jit_solution(2698235408975359406)
XLA Ops:
  0.6 0.0 copy-start
  0.6 0.0 copy-start.1
  0.7 3.3 %opening.1 = (f32[4,2,128,256]{3,2,1,0:T(8,128)S(1)}, f32[4,2,128,256]{3,2,1,0:T(8,128)}, f32[128,128]{1,0:T(8,128)}) custom-call(f32[4,16,128,256]{3,2,1,0:T(8,128)} %state.3, f32[2,1024]{1,0:T(2,128)} %angles.1, f32[1,1024]{1,0:T(1,128)} %bitcast.10, f32[1,1024]{1,0:T(1,128)} %bitcast.11, f32[1,1024]{1,0:T(1,128)} %bitcast.12), custom_call_target="tpu_custom_call" | custom-call | tf_op jit(solution)/shard_map/opening/pallas_call | solution.py:203
  4.0 2.8 %collective-permute-start = (f32[4,2,128,256]{3,2,1,0:T(8,128)}, f32[4,2,128,256]{3,2,1,0:T(8,128)S(1)}, u32[]{:S(2)}, u32[]{:S(2)}) collective-permute-start(f32[4,2,128,256]{3,2,1,0:T(8,128)} %get-tuple-element.12), channel_id=1, source_target_pairs={{0,1},{1,2},{2,3},{3,4},{4,5},{5,6},{6,7},{7,8},{8,9},{9,10},{10,1... | collective-permute-start | bytes 3145736 | tf_op jit(solution)/shard_map/ppermute | solution.py:491
  6.7 0.0 collective-permute-start.1
  6.7 10.6 %all-to-all-start = ((f32[128,1,128]{2,1,0:T(1,128)}), f32[128,1,128]{2,1,0:T(1,128)S(1)}, u32[]{:S(2)}, u32[]{:S(2)}) async-start(f32[128,1,128]{2,1,0:T(1,128)} %bitcast.9), calls=%async_computation | async-start | bytes 131072 | tf_op jit(solution)/shard_map/all_to_all | solution.py:493
  17.3 18.0 %interior.1 = (f32[21,2,4,136,128]{4,3,2,1,0:T(8,128)S(1)}, f32[19,2,4,136,128]{4,3,2,1,0:T(8,128)S(1)}, f32[4,16,128,256]{3,2,1,0:T(8,128)}) custom-call(f32[4,16,128,256]{3,2,1,0:T(8,128)} %state.3), custom_call_target="tpu_custom_call" | custom-call | tf_op jit(solution)/shard_map/interior/pallas_call | solution.py:288
  35.3 0.0 collective-permute-done.west_halo
  35.3 0.0 collective-permute-done.1.east_halo
  35.3 0.0 copy-done
  35.3 0.0 copy-done.1
  35.3 9.8 %edges.1 = (f32[21,2,4,136,128]{4,3,2,1,0:T(8,128)S(1)}, f32[19,2,4,136,128]{4,3,2,1,0:T(8,128)S(1)}, f32[4,16,128,256]{3,2,1,0:T(8,128)}, f32[4,8,128]{2,1,0:T(8,128)S(1)}) custom-call(s32[512]{0:T(512)S(1)} %copy-done.1, f32[3,512]{1,0:T(4,128)S(1)} %copy-done, ...), custom_call_target="tpu_custom_call", output_to_operand_aliasing={{0}: (2, {}), {1}: (3, {}), {2}: (6, {})} | custom-call | tf_op jit(solution)/shard_map/edges/pallas_call | solution.py:390
  45.1 0.0 all-to-all-done
  45.1 2.1 %walls.1 = f32[4,512]{1,0:T(4,128)} custom-call(s32[1,512]{1,0:T(1,128)} %bitcast.13, f32[128,128]{1,0:T(8,128)S(1)} %bitcast.8, f32[4,8,128]{2,1,0:T(8,128)S(1)} %get-tuple-element.17.sampled), custom_call_target="tpu_custom_call" | custom-call | tf_op jit(solution)/shard_map/walls/pallas_call | solution.py:473
Async XLA Ops:
  0.6 34.6 %copy-start = (f32[3,512]{1,0:T(4,128)S(1)}, f32[3,512]{1,0:T(4,128)}, u32[]{:S(2)}) copy-start(f32[3,512]{1,0:T(4,128)} %fracs.1) | copy-start | bytes 18436
  0.6 34.6 %copy-start.1 = (s32[512]{0:T(512)S(1)}, s32[512]{0:T(512)}, u32[]{:S(2)}) copy-start(s32[512]{0:T(512)} %cells.1) | copy-start | bytes 6148
  4.0 31.3 %collective-permute-start = (f32[4,2,128,256]{3,2,1,0:T(8,128)}, f32[4,2,128,256]{3,2,1,0:T(8,128)S(1)}, u32[]{:S(2)}, u32[]{:S(2)}) collective-permute-start(f32[4,2,128,256]{3,2,1,0:T(8,128)} %get-tuple-element.12), channel_id=1, source_target_pairs={{0,1},{1,2},{2,3},{3,4},{4,5},{5,6},{6,7},{7,8},{8,9},{9,10},{10,1... | collective-permute-start | bytes 3145736 | tf_op jit(solution)/shard_map/ppermute | solution.py:491
  6.7 28.5 %collective-permute-start.1 = (f32[4,2,128,256]{3,2,1,0:T(8,128)S(1)}, f32[4,2,128,256]{3,2,1,0:T(8,128)S(1)}, u32[]{:S(2)}, u32[]{:S(2)}) collective-permute-start(f32[4,2,128,256]{3,2,1,0:T(8,128)S(1)} %get-tuple-element.13), channel_id=1, source_target_pairs={{1,0},{2,1},{3,2},{4,3},{5,4},{6,5},{7,6},{8,7},{9,8},{10,9},{11,1... | collective-permute-start | bytes 3145736 | tf_op jit(solution)/shard_map/ppermute | solution.py:492
  6.7 38.3 %all-to-all-start = ((f32[128,1,128]{2,1,0:T(1,128)}), f32[128,1,128]{2,1,0:T(1,128)S(1)}, u32[]{:S(2)}, u32[]{:S(2)}) async-start(f32[128,1,128]{2,1,0:T(1,128)} %bitcast.9), calls=%async_computation | async-start | bytes 131072 | tf_op jit(solution)/shard_map/all_to_all | solution.py:493

commit v3 on v2

--- a/solution.py
+++ b/solution.py
@@ -92,42 +92,43 @@
     return (xs + ys) + zs
 
 
-def middle_tile(s, m, su, sl, x, yb):
+def middle_tile(s, su, sl, shift_base, x, yb):
     b = base_of(x + 2, yb)
     center = load8a(s, b, PITCH)
     sides = (
         (load8a(s, b + LAYER, PITCH), load8a(s, b - LAYER, PITCH)),
         (load8(s, b + 1, PITCH), load8(s, b - 1, PITCH)),
-        (load8a(su, yb * 8, NY), load8a(sl, yb * 8, NY)),
+        (load8a(su, shift_base + yb * 8, NY), load8a(sl, shift_base + yb * 8, NY)),
     )
     coefs = coefficients(center, time_step)
     keep = 1.0 - 6.0 * grid_viscosity * time_step
-    tiles = [[blend(sides, h, c, coefs) + keep * center[h][c] for c in range(COMPS)] for h in range(HALVES)]
-    store8(m, base_of(x + 1, yb), PITCH, tiles)
-
-
-def final_tile(s, m, f, f_base, mu, ml, x, yb):
+    return [[blend(sides, h, c, coefs) + keep * center[h][c] for c in range(COMPS)] for h in range(HALVES)]
+
+
+def final_tile(s, m, mu, ml, shift_base, x, yb, east=None):
     b = base_of(x + 1, yb)
     center = load8a(m, b, PITCH)
     sides = (
-        (load8a(m, b + LAYER, PITCH), load8a(m, b - LAYER, PITCH)),
+        (load8a(m, b + LAYER, PITCH) if east is None else east, load8a(m, b - LAYER, PITCH)),
         (load8(m, b + 1, PITCH), load8(m, b - 1, PITCH)),
-        (load8a(mu, yb * 8, NY), load8a(ml, yb * 8, NY)),
+        (load8a(mu, shift_base + yb * 8, NY), load8a(ml, shift_base + yb * 8, NY)),
     )
     coefs = coefficients(center, 0.5 * time_step)
     keep = 0.5 - 3.0 * grid_viscosity * time_step
     old = load8a(s, base_of(x + 2, yb), PITCH)
-    tiles = [
+    return [
         [blend(sides, h, c, coefs) + (keep * center[h][c] + 0.5 * old[h][c]) for c in range(COMPS)]
         for h in range(HALVES)
     ]
-    store8(f, f_base + yb * 8, NY, tiles)
-
-
-def roll_tile(field, layer, yb, u_ref, l_ref):
-    u, l = shifted(load8a(field, base_of(layer, yb), PITCH))
-    store8(u_ref, yb * 8, NY, u)
-    store8(l_ref, yb * 8, NY, l)
+
+
+def shifted_tile(field, layer, yb):
+    return shifted(load8a(field, base_of(layer, yb), PITCH))
+
+
+def store_shifted(u_ref, l_ref, base, pair):
+    store8(u_ref, base, NY, pair[0])
+    store8(l_ref, base, NY, pair[1])
 
 
 def zero_pads(ref, layers):
@@ -214,9 +215,7 @@
     )(in_hbm(state), angles, height, temp, visc)
 
 
-def interior(
-    state, S, M, final, F, SU0, SL0, SU1, SL1, MU0, ML0, MU1, ML1, in_sem, out_sem
-):
+def interior(state, S, M, final, F, SU, SL, MU, ML, in_sem, out_sem):
     def in_copy(x, h):
         return pltpu.make_async_copy(half_layer(state, x, h), S.at[x + 2, h, :, pl.ds(8, NY), :], in_sem.at[x, h])
 
@@ -231,9 +230,6 @@
     s = S.reshape((CX + 5) * LAYER, LANES)
     m = M.reshape((CX + 3) * LAYER, LANES)
     f = F.reshape((CX - 4) * SHEET, LANES)
-    state_rolled = ((SU0, SL0), (SU1, SL1))
-    mid_rolled = ((MU0, ML0), (MU1, ML1))
-
     def landed(x):
         for h in range(HALVES):
             in_copy(x, h).wait()
@@ -241,43 +237,35 @@
     landed(0)
     landed(1)
     for yb in range(TILES):
-        roll_tile(s, 3, yb, *state_rolled[1])
-
-    def step(x, y, odd_x, odd_y, next_mid=None):
+        store_shifted(SU, SL, yb * 8, shifted_tile(s, 3, yb))
+
+    def sweep(x, with_final):
+        landed(x + 1)
+        mids = [middle_tile(s, SU, SL, 0, x, yb) for yb in range(TILES)]
+        if with_final:
+            rb = ((x - 1) & 1) * SHEET
+            fins = [final_tile(s, m, MU, ML, rb, x - 1, yb, mids[yb]) for yb in range(TILES)]
+        news = [shifted_tile(s, x + 3, yb) for yb in range(TILES)]
         for yb in range(TILES):
-            if y is not None:
-                final_tile(s, m, f, (y - 2) * SHEET, *mid_rolled[odd_y], y, yb)
-            if next_mid is not None:
-                roll_tile(m, next_mid + 1, yb, *mid_rolled[0 if y is None else 1 - odd_y])
-        for yb in range(TILES):
-            if x is not None:
-                middle_tile(s, m, *state_rolled[odd_x], x, yb)
-                roll_tile(s, x + 3, yb, *state_rolled[1 - odd_x])
-        if y is not None:
+            store8(m, base_of(x + 1, yb), PITCH, mids[yb])
+            if with_final:
+                store8(f, (x - 3) * SHEET + yb * 8, NY, fins[yb])
+            store_shifted(SU, SL, yb * 8, news[yb])
+            store_shifted(MU, ML, (x & 1) * SHEET + yb * 8, shifted(mids[yb]))
+        if with_final:
             for h in range(HALVES):
-                out_copy(y, h).start()
-
-    landed(2)
-    step(1, None, 1, 0)
-    landed(3)
-    step(2, None, 0, 0)
-    landed(4)
-    step(3, None, 1, 0)
-    landed(5)
-    step(4, None, 0, 0, next_mid=2)
-
-    def both(p, carry):
-        x = 5 + 2 * p
-        y = x - LAG
-        landed(x + 1)
-        step(x, y, 1, 0, next_mid=y + 1)
-        landed(x + 2)
-        step(x + 1, y + 1, 0, 1, next_mid=y + 2)
+                out_copy(x - 1, h).start()
+
+    def head(x, carry):
+        sweep(x, False)
         return carry
 
-    lax.fori_loop(0, (CX - 6) // 2, both, 0)
-    step(None, CX - 4, 0, 0, next_mid=CX - 3)
-    step(None, CX - 3, 0, 1)
+    def main(x, carry):
+        sweep(x, True)
+        return carry
+
+    lax.fori_loop(1, 3, head, 0)
+    lax.fori_loop(3, CX - 1, main, 0)
     for y in range(2, CX - 2):
         for h in range(HALVES):
             out_copy(y, h).wait()
@@ -294,8 +282,8 @@
         ),
         in_specs=[hbm_spec],
         out_specs=(vmem_spec, vmem_spec, hbm_spec),
-        scratch_shapes=[pltpu.VMEM((CX - 4, HALVES, COMPS, NY, LANES), f32)]
-        + [sheet] * 8
+        scratch_shapes=[pltpu.VMEM((CX - 4, HALVES, COMPS, NY, LANES), f32), sheet, sheet]
+        + [pltpu.VMEM((2 * SHEET, LANES), f32)] * 2
         + [pltpu.SemaphoreType.DMA((CX, 2)), pltpu.SemaphoreType.DMA((CX - 4, 2))],
         compiler_params=pltpu.CompilerParams(vmem_limit_bytes=14 << 20),
         name="interior",
@@ -321,29 +309,35 @@
     f = F.reshape(4 * SHEET, LANES)
     rolled = ((SU0, SL0), (SU1, SL1))
 
+    def put_middle(su, sl, x, yb):
+        store8(m, base_of(x + 1, yb), PITCH, middle_tile(s, su, sl, 0, x, yb))
+
+    def put_shifted(field, layer, yb, u_ref, l_ref):
+        store_shifted(u_ref, l_ref, yb * 8, shifted_tile(field, layer, yb))
+
     def mid_refs(n):
         return MU.at[pl.ds(n * SHEET, SHEET)], ML.at[pl.ds(n * SHEET, SHEET)]
 
     for yb in range(TILES):
-        roll_tile(s, 2, yb, *rolled[0])
-        roll_tile(m, 2, yb, *mid_refs(1))
+        put_shifted(s, 2, yb, *rolled[0])
+        put_shifted(m, 2, yb, *mid_refs(1))
     for k in range(4):
         for h in range(HALVES):
             in_copy(k, h).wait()
     for yb in range(TILES):
-        middle_tile(s, m, *rolled[0], 0, yb)
-        roll_tile(s, CX + 1, yb, *rolled[1])
-        roll_tile(m, CX - 1, yb, *mid_refs(2))
+        put_middle(*rolled[0], 0, yb)
+        put_shifted(s, CX + 1, yb, *rolled[1])
+        put_shifted(m, CX - 1, yb, *mid_refs(2))
     for yb in range(TILES):
-        middle_tile(s, m, *rolled[1], CX - 1, yb)
-        roll_tile(s, 1, yb, *rolled[0])
-        roll_tile(m, 1, yb, *mid_refs(0))
+        put_middle(*rolled[1], CX - 1, yb)
+        put_shifted(s, 1, yb, *rolled[0])
+        put_shifted(m, 1, yb, *mid_refs(0))
     for yb in range(TILES):
-        middle_tile(s, m, *rolled[0], -1, yb)
-        roll_tile(s, CX + 2, yb, *rolled[1])
-        roll_tile(m, CX, yb, *mid_refs(3))
+        put_middle(*rolled[0], -1, yb)
+        put_shifted(s, CX + 2, yb, *rolled[1])
+        put_shifted(m, CX, yb, *mid_refs(3))
     for yb in range(TILES):
-        middle_tile(s, m, *rolled[1], CX, yb)
+        put_middle(*rolled[1], CX, yb)
 
     def final_layer(n):
         return (n & 1) + (n >> 1) * (CX - 2)
@@ -371,7 +365,8 @@
         total = jnp.zeros((8, LANES), jnp.float32)
         per = LANES // TILES
         for yb in range(TILES):
-            final_tile(s, m, f, n * SHEET, *mid_refs(n), final_layer(n), yb)
+            tile = final_tile(s, m, MU, ML, n * SHEET, final_layer(n), yb)
+            store8(f, n * SHEET + yb * 8, NY, tile)
             for p in range(yb * per, yb * per + per):
                 total = jnp.where(lane == p, sampled_at(n * LANES + p), total)
         sampled[n] = total

time: 47.4 us -> 45.9 us (0.968)
  Pallas kernels: 33.1 us -> 31.6 us
    pallas_call x1, Pallas kernels: 18 us -> 16.4 us  [run_interior(): pl.pallas_call(interior, out_shape=(pltpu.VMEM(S_SHAPE, f32), pltpu.VMEM(...]
  transfers between devices with their start and end apart: 3 -> 3, of which waited for: 0 -> 0; matrix products, arithmetic and copies ran while one was open for 0% -> 0% of each run, Pallas kernels for 59% -> 57%
where the time goes in v3:
time: 45.9 us; the launch traced here: 45.7 us
  Pallas kernels  31.6 us (69%)
  starting transfers between devices  13.3 us (29%)
  between operations  0.72 us (2%)
    pallas_call x1, Pallas kernels, run_interior(): pl.pallas_call(interior, out_shape=(pltpu.VMEM(S_SHAPE, f32), pltpu.VMEM(...  16.4 us
    all_to_all x1, starting transfers between devices, on_device(): lax.all_to_all(packed, 'blk', split_axis=0, concat_axis=0, tiled=True)  10.6 us
    pallas_call x1, Pallas kernels, run_edges(): pl.pallas_call(edges, out_shape=(pltpu.VMEM(S_SHAPE, f32), pltpu.VMEM(M_S...  9.76 us
    pallas_call x1, Pallas kernels, run_opening(): pl.pallas_call(opening, out_shape=(pltpu.VMEM(RIM_SHAPE, f32), pltpu.VMEM...  3.32 us
    ppermute x1, starting transfers between devices, on_device(): west_halo = lax.ppermute(to_east, 'blk', ahead)  2.76 us
    pallas_call x1, Pallas kernels, run_walls(): pl.pallas_call(walls, out_shape=jax.ShapeDtypeStruct((COMPS, POINTS), jnp...  2.12 us
  transfers between devices with their start and end apart: 3, of which 0 were waited for; matrix products, arithmetic and copies ran while one was open for 0% of the time, Pallas kernels for 57%

profile of v3, /device:TPU:1, one launch (start us, length us, event | category | flops | bytes accessed | tf_op | source)
XLA Modules:
  0.0 45.7 jit_solution(15855078505225192927)
XLA Ops:
  0.6 0.0 copy-start
  0.6 0.0 copy-start.1
  0.7 3.3 %opening.1 = (f32[4,2,128,256]{3,2,1,0:T(8,128)S(1)}, f32[4,2,128,256]{3,2,1,0:T(8,128)}, f32[128,128]{1,0:T(8,128)}) custom-call(f32[4,16,128,256]{3,2,1,0:T(8,128)} %state.3, f32[2,1024]{1,0:T(2,128)} %angles.1, f32[1,1024]{1,0:T(1,128)} %bitcast.10, f32[1,1024]{1,0:T(1,128)} %bitcast.11, f32[1,1024]{1,0:T(1,128)} %bitcast.12), custom_call_target="tpu_custom_call" | custom-call | tf_op jit(solution)/shard_map/opening/pallas_call | solution.py:204
  4.0 2.8 %collective-permute-start = (f32[4,2,128,256]{3,2,1,0:T(8,128)}, f32[4,2,128,256]{3,2,1,0:T(8,128)S(1)}, u32[]{:S(2)}, u32[]{:S(2)}) collective-permute-start(f32[4,2,128,256]{3,2,1,0:T(8,128)} %get-tuple-element.12), channel_id=1, source_target_pairs={{0,1},{1,2},{2,3},{3,4},{4,5},{5,6},{6,7},{7,8},{8,9},{9,10},{10,1... | collective-permute-start | bytes 3145736 | tf_op jit(solution)/shard_map/ppermute | solution.py:486
  6.7 0.0 collective-permute-start.1
  6.7 10.6 %all-to-all-start = ((f32[128,1,128]{2,1,0:T(1,128)}), f32[128,1,128]{2,1,0:T(1,128)S(1)}, u32[]{:S(2)}, u32[]{:S(2)}) async-start(f32[128,1,128]{2,1,0:T(1,128)} %bitcast.9), calls=%async_computation | async-start | bytes 131072 | tf_op jit(solution)/shard_map/all_to_all | solution.py:488
  17.3 16.4 %interior.1 = (f32[21,2,4,136,128]{4,3,2,1,0:T(8,128)S(1)}, f32[19,2,4,136,128]{4,3,2,1,0:T(8,128)S(1)}, f32[4,16,128,256]{3,2,1,0:T(8,128)}) custom-call(f32[4,16,128,256]{3,2,1,0:T(8,128)} %state.3), custom_call_target="tpu_custom_call" | custom-call | tf_op jit(solution)/shard_map/interior/pallas_call | solution.py:276
  33.8 0.0 collective-permute-done.west_halo
  33.8 0.0 collective-permute-done.1.east_halo
  33.8 0.0 copy-done
  33.8 0.0 copy-done.1
  33.8 9.8 %edges.1 = (f32[21,2,4,136,128]{4,3,2,1,0:T(8,128)S(1)}, f32[19,2,4,136,128]{4,3,2,1,0:T(8,128)S(1)}, f32[4,16,128,256]{3,2,1,0:T(8,128)}, f32[4,8,128]{2,1,0:T(8,128)S(1)}) custom-call(s32[512]{0:T(512)S(1)} %copy-done.1, f32[3,512]{1,0:T(4,128)S(1)} %copy-done, ...), custom_call_target="tpu_custom_call", output_to_operand_aliasing={{0}: (2, {}), {1}: (3, {}), {2}: (6, {})} | custom-call | tf_op jit(solution)/shard_map/edges/pallas_call | solution.py:385
  43.6 0.0 all-to-all-done
  43.6 2.1 %walls.1 = f32[4,512]{1,0:T(4,128)} custom-call(s32[1,512]{1,0:T(1,128)} %bitcast.13, f32[128,128]{1,0:T(8,128)S(1)} %bitcast.8, f32[4,8,128]{2,1,0:T(8,128)S(1)} %get-tuple-element.17.sampled), custom_call_target="tpu_custom_call" | custom-call | tf_op jit(solution)/shard_map/walls/pallas_call | solution.py:468
Async XLA Ops:
  0.6 33.1 %copy-start = (f32[3,512]{1,0:T(4,128)S(1)}, f32[3,512]{1,0:T(4,128)}, u32[]{:S(2)}) copy-start(f32[3,512]{1,0:T(4,128)} %fracs.1) | copy-start | bytes 18436
  0.6 33.1 %copy-start.1 = (s32[512]{0:T(512)S(1)}, s32[512]{0:T(512)}, u32[]{:S(2)}) copy-start(s32[512]{0:T(512)} %cells.1) | copy-start | bytes 6148
  4.0 29.8 %collective-permute-start = (f32[4,2,128,256]{3,2,1,0:T(8,128)}, f32[4,2,128,256]{3,2,1,0:T(8,128)S(1)}, u32[]{:S(2)}, u32[]{:S(2)}) collective-permute-start(f32[4,2,128,256]{3,2,1,0:T(8,128)} %get-tuple-element.12), channel_id=1, source_target_pairs={{0,1},{1,2},{2,3},{3,4},{4,5},{5,6},{6,7},{7,8},{8,9},{9,10},{10,1... | collective-permute-start | bytes 3145736 | tf_op jit(solution)/shard_map/ppermute | solution.py:486
  6.7 27.0 %collective-permute-start.1 = (f32[4,2,128,256]{3,2,1,0:T(8,128)S(1)}, f32[4,2,128,256]{3,2,1,0:T(8,128)S(1)}, u32[]{:S(2)}, u32[]{:S(2)}) collective-permute-start(f32[4,2,128,256]{3,2,1,0:T(8,128)S(1)} %get-tuple-element.13), channel_id=1, source_target_pairs={{1,0},{2,1},{3,2},{4,3},{5,4},{6,5},{7,6},{8,7},{9,8},{10,9},{11,1... | collective-permute-start | bytes 3145736 | tf_op jit(solution)/shard_map/ppermute | solution.py:487
  6.7 36.8 %all-to-all-start = ((f32[128,1,128]{2,1,0:T(1,128)}), f32[128,1,128]{2,1,0:T(1,128)S(1)}, u32[]{:S(2)}, u32[]{:S(2)}) async-start(f32[128,1,128]{2,1,0:T(1,128)} %bitcast.9), calls=%async_computation | async-start | bytes 131072 | tf_op jit(solution)/shard_map/all_to_all | solution.py:488

commit v4 on v3

--- a/solution.py
+++ b/solution.py
@@ -184,19 +184,25 @@
     )
 
 
-def opening(state, angles, height, temp, visc, to_west, to_east, packed, rim_sem):
+def opening(state, angles, height, temp, visc, to_west, to_east, packed, stage, rim_sem, out_sem):
     def rim_copy(k, c):
         if k == 0:
             return pltpu.make_async_copy(state.at[c, pl.ds(0, 2)], to_west.at[c], rim_sem.at[0, c])
-        return pltpu.make_async_copy(state.at[c, pl.ds(CX - 2, 2)], to_east.at[c], rim_sem.at[1, c])
-
-    for k in range(2):
+        return pltpu.make_async_copy(state.at[c, pl.ds(CX - 2, 2)], stage.at[c], rim_sem.at[1, c])
+
+    def out_copy(c):
+        return pltpu.make_async_copy(stage.at[c], to_east.at[c], out_sem.at[c])
+
+    for k in (1, 0):
         for c in range(COMPS):
             rim_copy(k, c).start()
+    for c in range(COMPS):
+        rim_copy(1, c).wait()
+        out_copy(c).start()
     packed[...] = packed_faces([angles[0:1, :], angles[1:2, :], height[...], temp[...], visc[...]])
-    for k in range(2):
-        for c in range(COMPS):
-            rim_copy(k, c).wait()
+    for c in range(COMPS):
+        rim_copy(0, c).wait()
+        out_copy(c).wait()
 
 
 def run_opening(state, angles, height, temp, visc):
@@ -205,12 +211,16 @@
         opening,
         out_shape=(
             pltpu.VMEM(RIM_SHAPE, f32),
-            pltpu.VMEM(RIM_SHAPE, f32),
+            jax.ShapeDtypeStruct(RIM_SHAPE, f32),
             jax.ShapeDtypeStruct((LANES, LANES), f32),
         ),
         in_specs=[hbm_spec, vmem_spec, vmem_spec, vmem_spec, vmem_spec],
-        out_specs=(vmem_spec, vmem_spec, vmem_spec),
-        scratch_shapes=[pltpu.SemaphoreType.DMA((2, COMPS))],
+        out_specs=(vmem_spec, hbm_spec, vmem_spec),
+        scratch_shapes=[
+            pltpu.VMEM(RIM_SHAPE, f32),
+            pltpu.SemaphoreType.DMA((2, COMPS)),
+            pltpu.SemaphoreType.DMA((COMPS,)),
+        ],
         name="opening",
     )(in_hbm(state), angles, height, temp, visc)
 

time: 45.9 us -> 46 us (level)
  no operation moved by 1% of the time
where the time goes in v4:
time: 46 us; the launch traced here: 45.8 us
  Pallas kernels  31.7 us (69%)
  starting transfers between devices  13.3 us (29%)
  between operations  0.72 us (2%)
    pallas_call x1, Pallas kernels, run_interior(): pl.pallas_call(interior, out_shape=(pltpu.VMEM(S_SHAPE, f32), pltpu.VMEM(...  16.4 us
    all_to_all x1, starting transfers between devices, on_device(): lax.all_to_all(packed, 'blk', split_axis=0, concat_axis=0, tiled=True)  10.6 us
    pallas_call x1, Pallas kernels, run_edges(): pl.pallas_call(edges, out_shape=(pltpu.VMEM(S_SHAPE, f32), pltpu.VMEM(M_S...  9.76 us
    pallas_call x1, Pallas kernels, run_opening(): pl.pallas_call(opening, out_shape=(pltpu.VMEM(RIM_SHAPE, f32), jax.ShapeD...  3.39 us
    ppermute x1, starting transfers between devices, on_device(): west_halo = lax.ppermute(to_east, 'blk', ahead)  2.76 us
    pallas_call x1, Pallas kernels, run_walls(): pl.pallas_call(walls, out_shape=jax.ShapeDtypeStruct((COMPS, POINTS), jnp...  2.12 us
  transfers between devices with their start and end apart: 3, of which 0 were waited for; matrix products, arithmetic and copies ran while one was open for 0% of the time, Pallas kernels for 57%

profile of v4, /device:TPU:1, one launch (start us, length us, event | category | flops | bytes accessed | tf_op | source)
XLA Modules:
  0.0 45.8 jit_solution(12452447882270626180)
XLA Ops:
  0.6 0.0 copy-start
  0.6 0.0 copy-start.1
  0.7 3.4 %opening.1 = (f32[4,2,128,256]{3,2,1,0:T(8,128)S(1)}, f32[4,2,128,256]{3,2,1,0:T(8,128)}, f32[128,128]{1,0:T(8,128)}) custom-call(f32[4,16,128,256]{3,2,1,0:T(8,128)} %state.3, f32[2,1024]{1,0:T(2,128)} %angles.1, f32[1,1024]{1,0:T(1,128)} %bitcast.10, f32[1,1024]{1,0:T(1,128)} %bitcast.11, f32[1,1024]{1,0:T(1,128)} %bitcast.12), custom_call_target="tpu_custom_call" | custom-call | tf_op jit(solution)/shard_map/opening/pallas_call | solution.py:210
  4.0 2.8 %collective-permute-start = (f32[4,2,128,256]{3,2,1,0:T(8,128)}, f32[4,2,128,256]{3,2,1,0:T(8,128)S(1)}, u32[]{:S(2)}, u32[]{:S(2)}) collective-permute-start(f32[4,2,128,256]{3,2,1,0:T(8,128)} %get-tuple-element.12), channel_id=1, source_target_pairs={{0,1},{1,2},{2,3},{3,4},{4,5},{5,6},{6,7},{7,8},{8,9},{9,10},{10,1... | collective-permute-start | bytes 3145736 | tf_op jit(solution)/shard_map/ppermute | solution.py:496
  6.8 0.0 collective-permute-start.1
  6.8 10.6 %all-to-all-start = ((f32[128,1,128]{2,1,0:T(1,128)}), f32[128,1,128]{2,1,0:T(1,128)S(1)}, u32[]{:S(2)}, u32[]{:S(2)}) async-start(f32[128,1,128]{2,1,0:T(1,128)} %bitcast.9), calls=%async_computation | async-start | bytes 131072 | tf_op jit(solution)/shard_map/all_to_all | solution.py:498
  17.4 16.4 %interior.1 = (f32[21,2,4,136,128]{4,3,2,1,0:T(8,128)S(1)}, f32[19,2,4,136,128]{4,3,2,1,0:T(8,128)S(1)}, f32[4,16,128,256]{3,2,1,0:T(8,128)}) custom-call(f32[4,16,128,256]{3,2,1,0:T(8,128)} %state.3), custom_call_target="tpu_custom_call" | custom-call | tf_op jit(solution)/shard_map/interior/pallas_call | solution.py:286
  33.8 0.0 collective-permute-done.west_halo
  33.8 0.0 collective-permute-done.1.east_halo
  33.8 0.0 copy-done
  33.9 0.0 copy-done.1
  33.9 9.8 %edges.1 = (f32[21,2,4,136,128]{4,3,2,1,0:T(8,128)S(1)}, f32[19,2,4,136,128]{4,3,2,1,0:T(8,128)S(1)}, f32[4,16,128,256]{3,2,1,0:T(8,128)}, f32[4,8,128]{2,1,0:T(8,128)S(1)}) custom-call(s32[512]{0:T(512)S(1)} %copy-done.1, f32[3,512]{1,0:T(4,128)S(1)} %copy-done, ...), custom_call_target="tpu_custom_call", output_to_operand_aliasing={{0}: (2, {}), {1}: (3, {}), {2}: (6, {})} | custom-call | tf_op jit(solution)/shard_map/edges/pallas_call | solution.py:395
  43.6 0.0 all-to-all-done
  43.6 2.1 %walls.1 = f32[4,512]{1,0:T(4,128)} custom-call(s32[1,512]{1,0:T(1,128)} %bitcast.13, f32[128,128]{1,0:T(8,128)S(1)} %bitcast.8, f32[4,8,128]{2,1,0:T(8,128)S(1)} %get-tuple-element.17.sampled), custom_call_target="tpu_custom_call" | custom-call | tf_op jit(solution)/shard_map/walls/pallas_call | solution.py:478
Async XLA Ops:
  0.6 33.2 %copy-start = (f32[3,512]{1,0:T(4,128)S(1)}, f32[3,512]{1,0:T(4,128)}, u32[]{:S(2)}) copy-start(f32[3,512]{1,0:T(4,128)} %fracs.1) | copy-start | bytes 18436
  0.6 33.2 %copy-start.1 = (s32[512]{0:T(512)S(1)}, s32[512]{0:T(512)}, u32[]{:S(2)}) copy-start(s32[512]{0:T(512)} %cells.1) | copy-start | bytes 6148
  4.0 29.8 %collective-permute-start = (f32[4,2,128,256]{3,2,1,0:T(8,128)}, f32[4,2,128,256]{3,2,1,0:T(8,128)S(1)}, u32[]{:S(2)}, u32[]{:S(2)}) collective-permute-start(f32[4,2,128,256]{3,2,1,0:T(8,128)} %get-tuple-element.12), channel_id=1, source_target_pairs={{0,1},{1,2},{2,3},{3,4},{4,5},{5,6},{6,7},{7,8},{8,9},{9,10},{10,1... | collective-permute-start | bytes 3145736 | tf_op jit(solution)/shard_map/ppermute | solution.py:496
  6.8 27.0 %collective-permute-start.1 = (f32[4,2,128,256]{3,2,1,0:T(8,128)S(1)}, f32[4,2,128,256]{3,2,1,0:T(8,128)S(1)}, u32[]{:S(2)}, u32[]{:S(2)}) collective-permute-start(f32[4,2,128,256]{3,2,1,0:T(8,128)S(1)} %get-tuple-element.13), channel_id=1, source_target_pairs={{1,0},{2,1},{3,2},{4,3},{5,4},{6,5},{7,6},{8,7},{9,8},{10,9},{11,1... | collective-permute-start | bytes 3145736 | tf_op jit(solution)/shard_map/ppermute | solution.py:497
  6.8 36.8 %all-to-all-start = ((f32[128,1,128]{2,1,0:T(1,128)}), f32[128,1,128]{2,1,0:T(1,128)S(1)}, u32[]{:S(2)}, u32[]{:S(2)}) async-start(f32[128,1,128]{2,1,0:T(1,128)} %bitcast.9), calls=%async_computation | async-start | bytes 131072 | tf_op jit(solution)/shard_map/all_to_all | solution.py:498
